TPU v7x, 256 devices: a whole 4x4x8 slice. The times are simulated.
256 devices in a mesh: wide: 32 (over x, y, core), narrow: 8 (over z).
Axes of the slice: x: 4, y: 4, z: 8, core: 2. Of those that a mesh axis runs over, the one named last changes fastest.
Arguments:
- panels: float32 [256, 512, 512], P('wide', 'narrow'), may hold values from -0.6 to 0.6
- factors: float32 [64, 512, 512], P('wide', 'narrow'), may hold values from -2 to 2
- member: int32 [64, 4], replicated, may hold values from 0 to 255, as said below
- target: int32 [64, 10], replicated, may hold values from 0 to 31
- ancestors: float32 [32, 512, 512], P('wide', 'narrow'), may hold values from -6 to 6
Outputs:
- updated: float32 [32, 512, 512], P('wide', 'narrow')
Inputs may be any that keep to these rules, and one draw needn't show every extreme that they name: `member`: the blocks of supernode s are 4 distinct indices in [(s // 2) * 8, (s // 2 + 1) * 8); every block belongs to exactly one supernode.
All inputs are finite; a program needn't handle non-finite values.
Results may differ from a plain program's by a relative error of at most 0.0003.
Values sent between devices are 32-bit elements; how exact they have to be, the bound alone decides.
No kernel may reach another device: no remote copies, remote signals or barrier semaphores. Data moves between devices by JAX's collectives and lax.ppermute only.
A program may use at most 128 MiB of HBM per device.

v0:
```python
import jax
import jax.numpy as jnp
from jax import lax
from jax.experimental import pallas as pl
from jax.experimental.pallas import tpu as pltpu
from jax.sharding import PartitionSpec as P


PAIRS = tuple((k, l) for k in range(4) for l in range(k + 1))
BOUNDS = (0, 4, 8)
CHUNKS = len(BOUNDS) - 1
SPOTS = tuple((c, b - BOUNDS[c]) for c in range(CHUNKS) for b in range(BOUNDS[c], BOUNDS[c + 1]))
ANY = pl.BlockSpec(memory_space=pltpu.HBM)
SMEM = pl.BlockSpec(memory_space=pltpu.SMEM)
VMEM = pl.BlockSpec(memory_space=pltpu.VMEM)
BF, F32 = jnp.bfloat16, jnp.float32


def split(x):
    high = x.astype(BF)
    return high, (x - high.astype(F32)).astype(BF)


def low_lanes(shape):
    return lax.broadcasted_iota(jnp.int32, shape, 1) < 64


def prepare(pos, member, target, meta):
    wide = pos[1]
    meta[0] = pos[0]
    meta[1] = wide & 1
    for s in range(2):
        for k in range(4):
            meta[2 + member[k, 2 * wide + s] - 8 * wide] = 4 * s + k
        for p in range(10):
            meta[10 + 10 * s + p] = target[p, 2 * wide + s]


def place(meta, s, p):
    tile = meta[10 + s * 10 + p]
    return (tile + meta[1]) & 1, tile >> 1


def scale(x_ref, f3, s):
    xh, xl = split(x_ref[pl.ds(4 * s, 4)].reshape(256, 512))
    x3 = jnp.concatenate([xh, xh, xl], axis=1)
    return split(lax.dot_general(x3, f3[s], (((1,), (0,)), ((), ())), preferred_element_type=F32))


def put(ref, index, parts):
    for i, part in enumerate(parts):
        ref[(*index, slice(None), pl.ds(512 * i, 512))] = part


def pairwise(left, right):
    return lax.dot_general(left, right, (((1,), (1,)), ((), ())), preferred_element_type=F32)


def tile_of(prod, k, l, upper):
    v = prod[pl.ds(k * 64, 64), pl.ds((l // 2) * 128, 128)]
    return v if (l % 2 == 1) == upper else pltpu.roll(v, 64, 1)


def folded(prod, k, l, lane):
    low, high = tile_of(prod, k, l, False), tile_of(prod, k, l, True)
    return jnp.where(lane, low[:32], high[32:])


def near_kernel(pos, member, target, *refs):
    *refs, meta = refs
    prepare(pos, member, target, meta)
    panels, up, down = refs[0], refs[1 : 1 + CHUNKS], refs[1 + CHUNKS : 1 + 2 * CHUNKS]
    fac = refs[1 + 2 * CHUNKS : 9 + 2 * CHUNKS]
    fu4 = refs[9 + 2 * CHUNKS]
    keep, send, f_out, n_out = refs[10 + 2 * CHUNKS : 14 + 2 * CHUNKS]
    x, f, f3, left, right, prod, acc, fsem, xsem, osem = refs[14 + 2 * CHUNKS :]
    z = meta[0]
    fcopies = []
    for i, (ref, d) in enumerate(zip(fac[:7], (0, -1, 1, -2, 2, -3, 3))):
        rows = pl.ds(pl.multiple_of(((z + d) & 7) * 64, 64), 64)
        fcopies.append(pltpu.make_async_copy(ref, f.at[:, rows], fsem.at[i]))
    rows4 = pl.ds(pl.multiple_of(((z + 4) & 7) * 64, 64), 64)
    fcopies.append(pltpu.make_async_copy(fu4, f.at[pl.ds(0, 1), rows4], fsem.at[7]))
    fcopies.append(pltpu.make_async_copy(fac[7], f.at[pl.ds(1, 1), rows4], fsem.at[8]))
    for c in fcopies:
        c.start()
    xcopies = []
    for piece in range(3):
        for b in range(8):
            src = panels.at[b] if piece == 0 else (up, down)[piece - 1][SPOTS[b][0]].at[SPOTS[b][1]]
            c = pltpu.make_async_copy(src, x.at[piece, meta[2 + b]], xsem.at[piece * 8 + b])
            c.start()
            xcopies.append(c)
    acc[...] = jnp.zeros_like(acc)
    for c in fcopies:
        c.wait()
    for s in range(2):
        high, low = split(f[s])
        for i, part in enumerate((high, low, high)):
            f3[s, pl.ds(512 * i, 512)] = part
    outs = [pltpu.make_async_copy(f3.at[:, pl.ds(0, 1024)], f_out, osem.at[0])]
    outs[0].start()
    for piece in range(3):
        for b in range(8):
            xcopies[piece * 8 + b].wait()
        for s in range(2):
            high, low = scale(x.at[piece], f3, s)
            put(left, (piece, s), (high, high, low))
            put(right, (piece, s), (high, low, high))
    outs.append(pltpu.make_async_copy(left.at[pl.ds(1, 2), :, :, pl.ds(512, 1024)], n_out, osem.at[1]))
    outs[1].start()
    lane = low_lanes((64, 128))
    for s in range(2):
        prod[0] = pairwise(left[0, s], right[1, s])
        prod[1] = pairwise(left[0, s], right[2, s])
        prod[2] = pairwise(left[2, s], right[1, s])
        prod[3] = pairwise(left[1, s], right[2, s])
        prod[4] = pairwise(left[0, s], right[0, s])
        for p, (k, l) in enumerate(PAIRS):
            side, chip = place(meta, s, p)
            for slot in range(2):
                low, high = tile_of(prod.at[2 * slot], k, l, False), tile_of(prod.at[2 * slot + 1], k, l, True)
                acc[side, chip, pl.ds(64 * slot, 64)] += jnp.where(lane, low, high)
            acc[side, chip, pl.ds(128, 32)] += folded(prod.at[4], k, l, lane[:32])
    outs += [pltpu.make_async_copy(acc.at[1], send, osem.at[2]), pltpu.make_async_copy(acc.at[0], keep, osem.at[3])]
    for c in outs[2:]:
        c.start()
    for c in outs:
        c.wait()


def far_kernel(pos, member, target, *refs):
    *refs, meta = refs
    prepare(pos, member, target, meta)
    up, down = refs[:CHUNKS], refs[CHUNKS : 2 * CHUNKS]
    f_in, n_in = refs[2 * CHUNKS : 2 + 2 * CHUNKS]
    keep, send = refs[2 + 2 * CHUNKS : 4 + 2 * CHUNKS]
    x, f3, near, left, right, prod, acc, isem, xsem, osem = refs[4 + 2 * CHUNKS :]
    copies = []
    ins = (
        (f_in, f3.at[:, pl.ds(0, 1024)]),
        (f_in.at[:, pl.ds(0, 512)], f3.at[:, pl.ds(1024, 512)]),
        (n_in, near.at[:, :, :, pl.ds(512, 1024)]),
        (n_in.at[:, :, :, pl.ds(0, 512)], near.at[:, :, :, pl.ds(0, 512)]),
    )
    xcopies = []
    for i, (a, b) in enumerate(ins):
        copies.append(pltpu.make_async_copy(a, b, isem.at[i]))
    for c in copies[:2]:
        c.start()
    for piece in range(2):
        for b in range(8):
            src = (up, down)[piece][SPOTS[b][0]].at[SPOTS[b][1]]
            c = pltpu.make_async_copy(src, x.at[piece, meta[2 + b]], xsem.at[piece * 8 + b])
            c.start()
            xcopies.append(c)
    for c in copies[2:]:
        c.start()
    acc[...] = jnp.zeros_like(acc)
    for c in copies[:2]:
        c.wait()
    for piece in range(2):
        for b in range(8):
            xcopies[piece * 8 + b].wait()
        for s in range(2):
            high, low = scale(x.at[piece], f3, s)
            if piece == 0:
                put(left, (s,), (high, high, low))
            put(right, (piece, s), (high, low, high))
    for c in copies[2:]:
        c.wait()
    lane = low_lanes((64, 128))
    for s in range(2):
        prod[0] = pairwise(left[s], right[1, s])
        prod[1] = pairwise(near[1, s], right[0, s])
        prod[2] = pairwise(near[0, s], right[1, s])
        for p, (k, l) in enumerate(PAIRS):
            side, chip = place(meta, s, p)
            acc[side, chip, pl.ds(64, 32)] += folded(prod.at[0], k, l, lane[:32])
            acc[side, chip, pl.ds(0, 64)] += jnp.where(lane, tile_of(prod.at[1], k, l, False), tile_of(prod.at[2], k, l, True))
    out = [pltpu.make_async_copy(acc.at[1], send, osem.at[0]), pltpu.make_async_copy(acc.at[0], keep, osem.at[1])]
    for c in out:
        c.start()
    for c in out:
        c.wait()


def final_kernel(meta, anc, near, eu, ed, far, du, dd, cd, out, acc):
    z = meta[0]
    acc[...] = jnp.zeros_like(acc)
    lane = lax.broadcasted_iota(jnp.int32, (64, 128), 1) // 64

    def add(src, half, d, rows):
        m = (z + d) & 7
        v = jnp.where((m & 1) == half, src, pltpu.roll(src, 64, 1))
        acc[m >> 1, rows] += jnp.where(lane[: v.shape[0]] == (m & 1), v, 0.0)

    every, top, bottom = pl.ds(0, 64), pl.ds(0, 32), pl.ds(32, 32)
    e1 = near[pl.ds(0, 64)]
    for src, half, d in ((e1, 0, -1), (e1, 1, 1), (eu[...], 0, -2), (ed[...], 1, 2), (du[...], 0, -3), (dd[...], 1, 3)):
        add(src, half, d, every)
    for src, d in ((near[pl.ds(128, 32)], 0), (cd[...], 4)):
        add(src, 0, d, top)
        add(src, 1, d, bottom)
    for q in range(4):
        cols = pl.ds(q * 128, 128)
        out[0, :, cols] = anc[0, :, cols] - acc[q]


def level(panels, factors, member, target, ancestors):
    wide = lax.axis_index("wide")
    z = lax.axis_index("narrow")
    scalars = (jnp.stack([z, wide]).astype(jnp.int32), member.T, target.T)

    def along(x, d):
        return lax.ppermute(x, "narrow", [(i, (i + d) % 8) for i in range(8)])

    def swap(x):
        return lax.ppermute(x, "wide", [(i, i ^ 1) for i in range(32)])

    def scatter(x):
        groups = [[2 * i + c for i in range(16)] for c in range(2)]
        return lax.all_to_all(x, "wide", 0, 0, axis_index_groups=groups, tiled=True)

    chunks = [panels[BOUNDS[c] : BOUNDS[c + 1]] for c in range(CHUNKS)]
    fu, fd = [factors], [factors]
    for _ in range(3):
        fu.append(along(fu[-1], 1))
        fd.append(along(fd[-1], -1))
    fu4 = along(fu[3][:1], 1)
    fd4 = along(fd[3][1:], -1)
    u1 = [along(c, 1) for c in chunks]
    d1 = [along(c, -1) for c in chunks]
    u2 = [along(c, 1) for c in u1]
    d2 = [along(c, -1) for c in d1]

    early = jax.ShapeDtypeStruct((16, 160, 128), F32)
    late = jax.ShapeDtypeStruct((16, 96, 128), F32)
    factor = jax.ShapeDtypeStruct((2, 1024, 512), BF)
    rows = jax.ShapeDtypeStruct((2, 2, 256, 1024), BF)
    dma = pltpu.SemaphoreType.DMA
    near = pl.pallas_call(
        near_kernel,
        name="near",
        out_shape=(early, early, factor, rows),
        in_specs=[SMEM] * 3 + [ANY] * (10 + 2 * CHUNKS),
        out_specs=(ANY,) * 4,
        scratch_shapes=[
            pltpu.VMEM((3, 8, 64, 512), F32),
            pltpu.VMEM((2, 512, 512), F32),
            pltpu.VMEM((2, 1536, 512), BF),
            pltpu.VMEM((3, 2, 256, 1536), BF),
            pltpu.VMEM((3, 2, 256, 1536), BF),
            pltpu.VMEM((5, 256, 256), F32),
            pltpu.VMEM((2, 16, 160, 128), F32),
            dma((9,)),
            dma((24,)),
            dma((4,)),
            pltpu.SMEM((30,), jnp.int32),
        ],
    )
    keep1, send1, f3, n3 = near(*scalars, panels, *u1, *d1, factors, fu[1], fd[1], fu[2], fd[2], fu[3], fd[3], fd4, fu4)
    r1 = jnp.sum(scatter(keep1 + swap(send1)), axis=0)
    eu, ed = along(r1[64:128], 1), along(r1[64:128], -1)

    far = pl.pallas_call(
        far_kernel,
        name="far",
        compiler_params=pltpu.CompilerParams(vmem_limit_bytes=24 << 20),
        out_shape=(late, late),
        in_specs=[SMEM] * 3 + [ANY] * (2 + 2 * CHUNKS),
        out_specs=(ANY,) * 2,
        scratch_shapes=[
            pltpu.VMEM((2, 8, 64, 512), F32),
            pltpu.VMEM((2, 1536, 512), BF),
            pltpu.VMEM((2, 2, 256, 1536), BF),
            pltpu.VMEM((2, 256, 1536), BF),
            pltpu.VMEM((2, 2, 256, 1536), BF),
            pltpu.VMEM((3, 256, 256), F32),
            pltpu.VMEM((2, 16, 96, 128), F32),
            dma((4,)),
            dma((16,)),
            dma((2,)),
            pltpu.SMEM((30,), jnp.int32),
        ],
    )
    keep2, send2 = far(*scalars, *u2, *d2, f3, n3)
    r2 = jnp.sum(scatter(keep2 + swap(send2)), axis=0)
    side, own = r2[:64], r2[64:]
    du, dd, cd = along(side, 1), along(side, -1), along(own, -2)
    return pl.pallas_call(
        final_kernel,
        name="final",
        out_shape=jax.ShapeDtypeStruct((1, 64, 512), F32),
        in_specs=[SMEM] + [VMEM] * 8,
        out_specs=VMEM,
        scratch_shapes=[pltpu.VMEM((4, 64, 128), F32)],
    )(scalars[0], ancestors, r1, eu, ed, r2, du, dd, cd)


def solution(mesh):
    return jax.shard_map(
        level,
        mesh=mesh,
        in_specs=(
            P("wide", "narrow", None),
            P("wide", "narrow", None),
            P(),
            P(),
            P("wide", "narrow", None),
        ),
        out_specs=P("wide", "narrow", None),
        check_vma=False,
    )
```

profile of v0, /device:TPU:2, one launch (start us, length us, event | category | flops | bytes accessed | tf_op | source)
XLA Modules:
  0.0 162.3 jit_solution(5987437548120624348)
XLA Ops:
  0.0 1.3 fusion
  1.4 2.0 %collective-permute-start = (f32[4,64,512]{2,1,0:T(8,128)S(1)}, f32[4,64,512]{2,1,0:T(8,128)S(1)}, u32[]{:S(2)}, u32[]{:S(2)}) collective-permute-start(f32[4,64,512]{2,1,0:T(8,128)S(1)} %get-tuple-element.18), channel_id=1, source_target_pairs={{0,1},{1,2},{2,3},{3,4},{4,5},{5,6},{6,7},{7,0},{8,9},{9,10},{10,1... | collective-permute-start | bytes 1572872 | tf_op jit(solution)/shard_map/ppermute | solution.py:216
  3.4 4.0 %collective-permute-start.5 = (f32[2,64,512]{2,1,0:T(8,128)S(1)}, f32[2,64,512]{2,1,0:T(8,128)S(1)}, u32[]{:S(2)}, u32[]{:S(2)}) collective-permute-start(f32[2,64,512]{2,1,0:T(8,128)S(1)} %copy-done.11), channel_id=1, source_target_pairs={{0,7},{1,0},{2,1},{3,2},{4,3},{5,4},{6,5},{7,6},{8,15},{9,8},{10,9... | collective-permute-start | bytes 786440 | tf_op jit(solution)/shard_map/ppermute | solution.py:216
  7.4 0.0 collective-permute-start.4
  7.4 0.0 collective-permute-start.1
  7.4 3.3 %collective-permute-start.2 = (f32[4,64,512]{2,1,0:T(8,128)S(1)}, f32[4,64,512]{2,1,0:T(8,128)}, u32[]{:S(2)}, u32[]{:S(2)}) collective-permute-start(f32[4,64,512]{2,1,0:T(8,128)S(1)} %get-tuple-element.18), channel_id=1, source_target_pairs={{0,7},{1,0},{2,1},{3,2},{4,3},{5,4},{6,5},{7,6},{8,15},{9,8},{10,9... | collective-permute-start | bytes 1572872 | tf_op jit(solution)/shard_map/ppermute | solution.py:216
  10.7 3.4 %collective-permute-done.5.refs_7_ = f32[2,64,512]{2,1,0:T(8,128)S(1)} collective-permute-done((f32[2,64,512]{2,1,0:T(8,128)S(1)}, f32[2,64,512]{2,1,0:T(8,128)S(1)}, u32[]{:S(2)}, u32[]{:S(2)}) %collective-permute-start.5) | collective-permute-done | bytes 262176 | tf_op jit(solution)/shard_map/ppermute | solution.py:216
  14.1 3.7 %collective-permute-start.3 = (f32[4,64,512]{2,1,0:T(8,128)S(1)}, f32[4,64,512]{2,1,0:T(8,128)}, u32[]{:S(2)}, u32[]{:S(2)}) collective-permute-start(f32[4,64,512]{2,1,0:T(8,128)S(1)} %get-tuple-element.17), channel_id=1, source_target_pairs={{0,7},{1,0},{2,1},{3,2},{4,3},{5,4},{6,5},{7,6},{8,15},{9,8},{10,9... | collective-permute-start | bytes 1572872 | tf_op jit(solution)/shard_map/ppermute | solution.py:216
  17.8 7.9 %collective-permute-done.4.refs_6_ = f32[2,64,512]{2,1,0:T(8,128)S(1)} collective-permute-done((f32[2,64,512]{2,1,0:T(8,128)S(1)}, f32[2,64,512]{2,1,0:T(8,128)S(1)}, u32[]{:S(2)}, u32[]{:S(2)}) %collective-permute-start.4) | collective-permute-done | bytes 262176 | tf_op jit(solution)/shard_map/ppermute | solution.py:216
  25.7 2.0 %collective-permute-start.7 = (f32[2,64,512]{2,1,0:T(8,128)S(1)}, f32[2,64,512]{2,1,0:T(8,128)S(1)}, u32[]{:S(2)}, u32[]{:S(2)}) collective-permute-start(f32[2,64,512]{2,1,0:T(8,128)S(1)} %collective-permute-done.5.refs_7_), channel_id=1, source_target_pairs={{0,7},{1,0},{2,1},{3,2},{4,3},{5,4},{6,5},{7,6},{8,15},{9,8},{10,9... | collective-permute-start | bytes 786440 | tf_op jit(solution)/shard_map/ppermute | solution.py:216
  27.7 0.0 collective-permute-done.refs_1_
  27.7 0.0 collective-permute-start.6
  27.7 13.3 %collective-permute-done.7.refs_9_ = f32[2,64,512]{2,1,0:T(8,128)S(1)} collective-permute-done((f32[2,64,512]{2,1,0:T(8,128)S(1)}, f32[2,64,512]{2,1,0:T(8,128)S(1)}, u32[]{:S(2)}, u32[]{:S(2)}) %collective-permute-start.7) | collective-permute-done | bytes 262176 | tf_op jit(solution)/shard_map/ppermute | solution.py:216
  41.0 3.7 %collective-permute-start.9 = (f32[2,64,512]{2,1,0:T(8,128)S(1)}, f32[2,64,512]{2,1,0:T(8,128)S(1)}, u32[]{:S(2)}, u32[]{:S(2)}) collective-permute-start(f32[2,64,512]{2,1,0:T(8,128)S(1)} %collective-permute-done.7.refs_9_), channel_id=1, source_target_pairs={{0,7},{1,0},{2,1},{3,2},{4,3},{5,4},{6,5},{7,6},{8,15},{9,8},{10,9... | collective-permute-start | bytes 786440 | tf_op jit(solution)/shard_map/ppermute | solution.py:216
  44.7 0.0 collective-permute-done.6.refs_8_
  44.7 0.1 collective-permute-start.8
  44.8 0.0 collective-permute-done.1.refs_2_
  44.8 0.1 collective-permute-start.15
  44.9 0.0 collective-permute-done.2.refs_3_
  44.9 2.6 %collective-permute-start.16 = (f32[4,64,512]{2,1,0:T(8,128)}, f32[4,64,512]{2,1,0:T(8,128)S(1)}, u32[]{:S(2)}, u32[]{:S(2)}) collective-permute-start(f32[4,64,512]{2,1,0:T(8,128)} %collective-permute-done.1.refs_2_), channel_id=1, source_target_pairs={{0,1},{1,2},{2,3},{3,4},{4,5},{5,6},{6,7},{7,0},{8,9},{9,10},{10,1... | collective-permute-start | bytes 1572872 | tf_op jit(solution)/shard_map/ppermute | solution.py:216
  47.5 0.0 collective-permute-done.3.refs_4_
  47.5 0.8 collective-permute-start.17
  48.3 3.2 %collective-permute-done.9.refs_11_ = f32[2,64,512]{2,1,0:T(8,128)S(1)} collective-permute-done((f32[2,64,512]{2,1,0:T(8,128)S(1)}, f32[2,64,512]{2,1,0:T(8,128)S(1)}, u32[]{:S(2)}, u32[]{:S(2)}) %collective-permute-start.9) | collective-permute-done | bytes 262176 | tf_op jit(solution)/shard_map/ppermute | solution.py:216
  51.4 3.7 %collective-permute-start.18 = (f32[4,64,512]{2,1,0:T(8,128)}, f32[4,64,512]{2,1,0:T(8,128)S(1)}, u32[]{:S(2)}, u32[]{:S(2)}) collective-permute-start(f32[4,64,512]{2,1,0:T(8,128)} %collective-permute-done.3.refs_4_), channel_id=1, source_target_pairs={{0,7},{1,0},{2,1},{3,2},{4,3},{5,4},{6,5},{7,6},{8,15},{9,8},{10,9... | collective-permute-start | bytes 1572872 | tf_op jit(solution)/shard_map/ppermute | solution.py:216
  55.1 0.1 collective-permute-done.8.refs_10_
  55.2 0.0 collective-permute-start.10
  55.3 0.7 slice.30
  56.0 18.7 %collective-permute-done.10.refs_12_ = f32[1,64,512]{2,1,0:T(8,128)S(1)} collective-permute-done((f32[1,64,512]{2,1,0:T(8,128)S(1)}, f32[1,64,512]{2,1,0:T(8,128)S(1)}, u32[]{:S(2)}, u32[]{:S(2)}) %collective-permute-start.10) | collective-permute-done | bytes 131104 | tf_op jit(solution)/shard_map/ppermute | solution.py:216
  74.7 1.7 %collective-permute-start.11 = (f32[1,64,512]{2,1,0:T(8,128)}, f32[1,64,512]{2,1,0:T(8,128)}, u32[]{:S(2)}, u32[]{:S(2)}) collective-permute-start(f32[1,64,512]{2,1,0:T(8,128)} %slice.30), channel_id=1, source_target_pairs={{0,1},{1,2},{2,3},{3,4},{4,5},{5,6},{6,7},{7,0},{8,9},{9,10},{10,1... | collective-permute-start | bytes 393224 | tf_op jit(solution)/shard_map/ppermute | solution.py:216
  76.4 0.6 pad_add_fusion.pos.meta
  77.0 4.7 %collective-permute-done.11.refs_13_ = f32[1,64,512]{2,1,0:T(8,128)} collective-permute-done((f32[1,64,512]{2,1,0:T(8,128)}, f32[1,64,512]{2,1,0:T(8,128)}, u32[]{:S(2)}, u32[]{:S(2)}) %collective-permute-start.11) | collective-permute-done | bytes 131104 | tf_op jit(solution)/shard_map/ppermute | solution.py:216
  81.7 0.0 copy-start.2
  81.7 0.0 copy-start.3
  81.7 11.5 %near.1 = (f32[16,160,128]{2,1,0:T(8,128)}, f32[16,160,128]{2,1,0:T(8,128)}, bf16[2,1024,512]{2,1,0:T(8,128)(2,1)}, bf16[2,2,256,1024]{3,2,1,0:T(8,128)(2,1)}) custom-call(s32[2]{0:T(128)} %pad_add_fusion.pos.meta, s32[4,64]{1,0:T(4,128)} %bitcast.6, s32[10,64]{1,0:T(8,128)} %bitcast.4, f32[8,64,512]{2,1,0:T(8,128)} %refs_0_.1, f32[4,64,512]{2,1,0:T(8,128)} %copy-done.8, ...), custom_call_target="tpu_custom_call" | custom-call | tf_op jit(solution)/shard_map/near/pallas_call | solution.py:262
  93.3 0.0 collective-permute-done.16.refs_1_
  93.3 0.0 collective-permute-done.17.refs_2_
  93.3 1.6 copy-done
  94.9 1.6 copy-done.1
  96.5 8.1 %far.1 = (f32[16,96,128]{2,1,0:T(8,128)S(1)}, f32[16,96,128]{2,1,0:T(8,128)S(1)}) custom-call(s32[2]{0:T(128)S(1)} %copy-done.4, s32[4,64]{1,0:T(4,128)S(1)} %bitcast.7, s32[10,64]{1,0:T(8,128)S(1)} %bitcast.5, f32[4,64,512]{2,1,0:T(8,128)S(1)} %collective-permute-done.15.refs_0_, f32[4,64,512]{2,1,0:T(8,128)S(1)} %collective-permute-done.16.refs_1_, ...), custom_call_target="tpu_custom_call" | custom-call | tf_op jit(solution)/shard_map/far/pallas_call | solution.py:287
  104.6 0.1 collective-permute-start.19
  104.7 0.5 collective-permute-start.12
  105.2 1.8 %collective-permute-done.19 = f32[16,96,128]{2,1,0:T(8,128)S(1)} collective-permute-done((f32[16,96,128]{2,1,0:T(8,128)S(1)}, f32[16,96,128]{2,1,0:T(8,128)S(1)}, u32[]{:S(2)}, u32[]{:S(2)}) %collective-permute-start.19) | collective-permute-done | bytes 786464 | tf_op jit(solution)/shard_map/ppermute | solution.py:219
  106.9 1.0 add.7
  107.9 7.6 %all-to-all-start.1 = ((f32[16,96,128]{2,1,0:T(8,128)}), f32[16,96,128]{2,1,0:T(8,128)S(1)}, u32[]{:S(2)}, u32[]{:S(2)}) async-start(f32[16,96,128]{2,1,0:T(8,128)} %add.7), calls=%async_computation.1 | async-start | bytes 1572864 | tf_op jit(solution)/shard_map/all_to_all | solution.py:223
  115.5 0.0 collective-permute-done.12
  115.5 1.3 add.6
  116.8 11.1 %all-to-all-done.1 = f32[16,96,128]{2,1,0:T(8,128)S(1)} async-done(((f32[16,96,128]{2,1,0:T(8,128)}), f32[16,96,128]{2,1,0:T(8,128)S(1)}, u32[]{:S(2)}, u32[]{:S(2)}) %all-to-all-start.1) | async-done | bytes 786464 | tf_op jit(solution)/shard_map/all_to_all | solution.py:223
  127.9 6.1 %all-to-all-start = ((f32[16,160,128]{2,1,0:T(8,128)}), f32[16,160,128]{2,1,0:T(8,128)S(1)}, u32[]{:S(2)}, u32[]{:S(2)}) async-start(f32[16,160,128]{2,1,0:T(8,128)} %add.6), calls=%async_computation | async-start | bytes 2621440 | tf_op jit(solution)/shard_map/all_to_all | solution.py:223
  134.1 0.1 collective-permute-start.20
  134.2 3.2 %collective-permute-start.21 = (f32[64,128]{1,0:T(8,128)S(1)}, f32[64,128]{1,0:T(8,128)S(1)}, u32[]{:S(2)}, u32[]{:S(2)}) collective-permute-start(f32[64,128]{1,0:T(8,128)S(1)} %slice.32), channel_id=1, source_target_pairs={{0,7},{1,0},{2,1},{3,2},{4,3},{5,4},{6,5},{7,6},{8,15},{9,8},{10,9... | collective-permute-start | bytes 98312 | tf_op jit(solution)/shard_map/ppermute | solution.py:216
  137.4 13.8 %all-to-all-done = f32[16,160,128]{2,1,0:T(8,128)S(1)} async-done(((f32[16,160,128]{2,1,0:T(8,128)}), f32[16,160,128]{2,1,0:T(8,128)S(1)}, u32[]{:S(2)}, u32[]{:S(2)}) %all-to-all-start) | async-done | bytes 1310752 | tf_op jit(solution)/shard_map/all_to_all | solution.py:223
  151.2 0.1 reduce_sum.18.near
  151.3 0.1 collective-permute-start.13
  151.4 3.2 %collective-permute-start.14 = (f32[64,128]{1,0:T(8,128)S(1)}, f32[64,128]{1,0:T(8,128)S(1)}, u32[]{:S(2)}, u32[]{:S(2)}) collective-permute-start(f32[64,128]{1,0:T(8,128)S(1)} %slice.31), channel_id=1, source_target_pairs={{0,7},{1,0},{2,1},{3,2},{4,3},{5,4},{6,5},{7,6},{8,15},{9,8},{10,9... | collective-permute-start | bytes 98312 | tf_op jit(solution)/shard_map/ppermute | solution.py:216
  154.6 0.2 collective-permute-start.22
  154.9 4.4 %collective-permute-done.22.cd = f32[32,128]{1,0:T(8,128)S(1)} collective-permute-done((f32[32,128]{1,0:T(8,128)S(1)}, f32[32,128]{1,0:T(8,128)S(1)}, u32[]{:S(2)}, u32[]{:S(2)}) %collective-permute-start.22) | collective-permute-done | bytes 16416 | tf_op jit(solution)/shard_map/ppermute | solution.py:216
  159.2 0.0 collective-permute-done.20.du
  159.3 0.0 collective-permute-done.21.dd
  159.3 0.0 collective-permute-done.13.eu
  159.3 0.5 copy-done.21
  159.8 0.0 copy-done.17
  159.9 0.0 copy-done.18
  159.9 0.6 copy-done.20
  160.5 1.8 %final.1 = f32[1,64,512]{2,1,0:T(8,128)} custom-call(s32[2]{0:T(128)} %pad_add_fusion.pos.meta, f32[1,64,512]{2,1,0:T(8,128)} %anc.1, f32[160,128]{1,0:T(8,128)} %copy-done.9, f32[64,128]{1,0:T(8,128)} %copy-done.19, f32[64,128]{1,0:T(8,128)} %copy-done.20, f32[96,128]{1,0:T(8,128)} %copy-done.10, f32[64,128]{1,0:T(8,128)} %copy-done.17, ...), custom_call_target="tpu_custom_call" | custom-call | tf_op jit(solution)/shard_map/final/pallas_call | solution.py:291
  (44 shorter events, 0.1 us)
Async XLA Ops:
  0.0 3.4 %copy-start.11 = (f32[2,64,512]{2,1,0:T(8,128)S(1)}, f32[2,64,512]{2,1,0:T(8,128)}, u32[]{:S(2)}) copy-start(f32[2,64,512]{2,1,0:T(8,128)} %refs_5_.1) | copy-start | bytes 786436
  1.4 26.4 %collective-permute-start = (f32[4,64,512]{2,1,0:T(8,128)S(1)}, f32[4,64,512]{2,1,0:T(8,128)S(1)}, u32[]{:S(2)}, u32[]{:S(2)}) collective-permute-start(f32[4,64,512]{2,1,0:T(8,128)S(1)} %get-tuple-element.18), channel_id=1, source_target_pairs={{0,1},{1,2},{2,3},{3,4},{4,5},{5,6},{6,7},{7,0},{8,9},{9,10},{10,1... | collective-permute-start | bytes 1572872 | tf_op jit(solution)/shard_map/ppermute | solution.py:216
  3.4 10.7 %collective-permute-start.5 = (f32[2,64,512]{2,1,0:T(8,128)S(1)}, f32[2,64,512]{2,1,0:T(8,128)S(1)}, u32[]{:S(2)}, u32[]{:S(2)}) collective-permute-start(f32[2,64,512]{2,1,0:T(8,128)S(1)} %copy-done.11), channel_id=1, source_target_pairs={{0,7},{1,0},{2,1},{3,2},{4,3},{5,4},{6,5},{7,6},{8,15},{9,8},{10,9... | collective-permute-start | bytes 786440 | tf_op jit(solution)/shard_map/ppermute | solution.py:216
  7.4 18.3 %collective-permute-start.4 = (f32[2,64,512]{2,1,0:T(8,128)S(1)}, f32[2,64,512]{2,1,0:T(8,128)S(1)}, u32[]{:S(2)}, u32[]{:S(2)}) collective-permute-start(f32[2,64,512]{2,1,0:T(8,128)S(1)} %copy-done.11), channel_id=1, source_target_pairs={{0,1},{1,2},{2,3},{3,4},{4,5},{5,6},{6,7},{7,0},{8,9},{9,10},{10,1... | collective-permute-start | bytes 786440 | tf_op jit(solution)/shard_map/ppermute | solution.py:216
  7.4 37.4 %collective-permute-start.1 = (f32[4,64,512]{2,1,0:T(8,128)S(1)}, f32[4,64,512]{2,1,0:T(8,128)}, u32[]{:S(2)}, u32[]{:S(2)}) collective-permute-start(f32[4,64,512]{2,1,0:T(8,128)S(1)} %get-tuple-element.17), channel_id=1, source_target_pairs={{0,1},{1,2},{2,3},{3,4},{4,5},{5,6},{6,7},{7,0},{8,9},{9,10},{10,1... | collective-permute-start | bytes 1572872 | tf_op jit(solution)/shard_map/ppermute | solution.py:216
  7.4 37.5 %collective-permute-start.2 = (f32[4,64,512]{2,1,0:T(8,128)S(1)}, f32[4,64,512]{2,1,0:T(8,128)}, u32[]{:S(2)}, u32[]{:S(2)}) collective-permute-start(f32[4,64,512]{2,1,0:T(8,128)S(1)} %get-tuple-element.18), channel_id=1, source_target_pairs={{0,7},{1,0},{2,1},{3,2},{4,3},{5,4},{6,5},{7,6},{8,15},{9,8},{10,9... | collective-permute-start | bytes 1572872 | tf_op jit(solution)/shard_map/ppermute | solution.py:216
  14.1 34.2 %copy-start.12 = (f32[2,64,512]{2,1,0:T(8,128)}, f32[2,64,512]{2,1,0:T(8,128)S(1)}, u32[]{:S(2)}) copy-start(f32[2,64,512]{2,1,0:T(8,128)S(1)} %collective-permute-done.5.refs_7_) | copy-start | bytes 786436
  14.1 33.4 %collective-permute-start.3 = (f32[4,64,512]{2,1,0:T(8,128)S(1)}, f32[4,64,512]{2,1,0:T(8,128)}, u32[]{:S(2)}, u32[]{:S(2)}) collective-permute-start(f32[4,64,512]{2,1,0:T(8,128)S(1)} %get-tuple-element.17), channel_id=1, source_target_pairs={{0,7},{1,0},{2,1},{3,2},{4,3},{5,4},{6,5},{7,6},{8,15},{9,8},{10,9... | collective-permute-start | bytes 1572872 | tf_op jit(solution)/shard_map/ppermute | solution.py:216
  25.7 19.1 %copy-start.13 = (f32[2,64,512]{2,1,0:T(8,128)}, f32[2,64,512]{2,1,0:T(8,128)S(1)}, u32[]{:S(2)}) copy-start(f32[2,64,512]{2,1,0:T(8,128)S(1)} %collective-permute-done.4.refs_6_) | copy-start | bytes 786436
  25.7 15.4 %collective-permute-start.7 = (f32[2,64,512]{2,1,0:T(8,128)S(1)}, f32[2,64,512]{2,1,0:T(8,128)S(1)}, u32[]{:S(2)}, u32[]{:S(2)}) collective-permute-start(f32[2,64,512]{2,1,0:T(8,128)S(1)} %collective-permute-done.5.refs_7_), channel_id=1, source_target_pairs={{0,7},{1,0},{2,1},{3,2},{4,3},{5,4},{6,5},{7,6},{8,15},{9,8},{10,9... | collective-permute-start | bytes 786440 | tf_op jit(solution)/shard_map/ppermute | solution.py:216
  27.7 54.0 %copy-start.8 = (f32[4,64,512]{2,1,0:T(8,128)}, f32[4,64,512]{2,1,0:T(8,128)S(1)}, u32[]{:S(2)}) copy-start(f32[4,64,512]{2,1,0:T(8,128)S(1)} %collective-permute-done.refs_1_) | copy-start | bytes 1572868
  27.7 17.0 %collective-permute-start.6 = (f32[2,64,512]{2,1,0:T(8,128)S(1)}, f32[2,64,512]{2,1,0:T(8,128)S(1)}, u32[]{:S(2)}, u32[]{:S(2)}) collective-permute-start(f32[2,64,512]{2,1,0:T(8,128)S(1)} %collective-permute-done.4.refs_6_), channel_id=1, source_target_pairs={{0,1},{1,2},{2,3},{3,4},{4,5},{5,6},{6,7},{7,0},{8,9},{9,10},{10,1... | collective-permute-start | bytes 786440 | tf_op jit(solution)/shard_map/ppermute | solution.py:216
  41.0 40.6 %copy-start.14 = (f32[2,64,512]{2,1,0:T(8,128)}, f32[2,64,512]{2,1,0:T(8,128)S(1)}, u32[]{:S(2)}) copy-start(f32[2,64,512]{2,1,0:T(8,128)S(1)} %collective-permute-done.7.refs_9_) | copy-start | bytes 786436
  41.0 10.4 %collective-permute-start.9 = (f32[2,64,512]{2,1,0:T(8,128)S(1)}, f32[2,64,512]{2,1,0:T(8,128)S(1)}, u32[]{:S(2)}, u32[]{:S(2)}) collective-permute-start(f32[2,64,512]{2,1,0:T(8,128)S(1)} %collective-permute-done.7.refs_9_), channel_id=1, source_target_pairs={{0,7},{1,0},{2,1},{3,2},{4,3},{5,4},{6,5},{7,6},{8,15},{9,8},{10,9... | collective-permute-start | bytes 786440 | tf_op jit(solution)/shard_map/ppermute | solution.py:216
  44.7 10.5 %copy-start.15 = (f32[2,64,512]{2,1,0:T(8,128)}, f32[2,64,512]{2,1,0:T(8,128)S(1)}, u32[]{:S(2)}) copy-start(f32[2,64,512]{2,1,0:T(8,128)S(1)} %collective-permute-done.6.refs_8_) | copy-start | bytes 786436
  44.7 10.5 %collective-permute-start.8 = (f32[2,64,512]{2,1,0:T(8,128)S(1)}, f32[2,64,512]{2,1,0:T(8,128)S(1)}, u32[]{:S(2)}, u32[]{:S(2)}) collective-permute-start(f32[2,64,512]{2,1,0:T(8,128)S(1)} %collective-permute-done.6.refs_8_), channel_id=1, source_target_pairs={{0,1},{1,2},{2,3},{3,4},{4,5},{5,6},{6,7},{7,0},{8,9},{9,10},{10,1... | collective-permute-start | bytes 786440 | tf_op jit(solution)/shard_map/ppermute | solution.py:216
  44.8 48.4 %collective-permute-start.15 = (f32[4,64,512]{2,1,0:T(8,128)S(1)}, f32[4,64,512]{2,1,0:T(8,128)S(1)}, u32[]{:S(2)}, u32[]{:S(2)}) collective-permute-start(f32[4,64,512]{2,1,0:T(8,128)S(1)} %collective-permute-done.refs_1_), channel_id=1, source_target_pairs={{0,1},{1,2},{2,3},{3,4},{4,5},{5,6},{6,7},{7,0},{8,9},{9,10},{10,1... | collective-permute-start | bytes 1572872 | tf_op jit(solution)/shard_map/ppermute | solution.py:216
  44.9 48.3 %collective-permute-start.16 = (f32[4,64,512]{2,1,0:T(8,128)}, f32[4,64,512]{2,1,0:T(8,128)S(1)}, u32[]{:S(2)}, u32[]{:S(2)}) collective-permute-start(f32[4,64,512]{2,1,0:T(8,128)} %collective-permute-done.1.refs_2_), channel_id=1, source_target_pairs={{0,1},{1,2},{2,3},{3,4},{4,5},{5,6},{6,7},{7,0},{8,9},{9,10},{10,1... | collective-permute-start | bytes 1572872 | tf_op jit(solution)/shard_map/ppermute | solution.py:216
  47.5 45.8 %collective-permute-start.17 = (f32[4,64,512]{2,1,0:T(8,128)}, f32[4,64,512]{2,1,0:T(8,128)S(1)}, u32[]{:S(2)}, u32[]{:S(2)}) collective-permute-start(f32[4,64,512]{2,1,0:T(8,128)} %collective-permute-done.2.refs_3_), channel_id=1, source_target_pairs={{0,7},{1,0},{2,1},{3,2},{4,3},{5,4},{6,5},{7,6},{8,15},{9,8},{10,9... | collective-permute-start | bytes 1572872 | tf_op jit(solution)/shard_map/ppermute | solution.py:216
  51.4 30.3 %copy-start.6 = (f32[2,64,512]{2,1,0:T(8,128)}, f32[2,64,512]{2,1,0:T(8,128)S(1)}, u32[]{:S(2)}) copy-start(f32[2,64,512]{2,1,0:T(8,128)S(1)} %collective-permute-done.9.refs_11_) | copy-start | bytes 786436
  51.4 41.8 %collective-permute-start.18 = (f32[4,64,512]{2,1,0:T(8,128)}, f32[4,64,512]{2,1,0:T(8,128)S(1)}, u32[]{:S(2)}, u32[]{:S(2)}) collective-permute-start(f32[4,64,512]{2,1,0:T(8,128)} %collective-permute-done.3.refs_4_), channel_id=1, source_target_pairs={{0,7},{1,0},{2,1},{3,2},{4,3},{5,4},{6,5},{7,6},{8,15},{9,8},{10,9... | collective-permute-start | bytes 1572872 | tf_op jit(solution)/shard_map/ppermute | solution.py:216
  55.2 26.5 %copy-start.7 = (f32[2,64,512]{2,1,0:T(8,128)}, f32[2,64,512]{2,1,0:T(8,128)S(1)}, u32[]{:S(2)}) copy-start(f32[2,64,512]{2,1,0:T(8,128)S(1)} %collective-permute-done.8.refs_10_) | copy-start | bytes 786436
  55.2 19.5 %collective-permute-start.10 = (f32[1,64,512]{2,1,0:T(8,128)S(1)}, f32[1,64,512]{2,1,0:T(8,128)S(1)}, u32[]{:S(2)}, u32[]{:S(2)}) collective-permute-start(f32[1,64,512]{2,1,0:T(8,128)S(1)} %slice.29), channel_id=1, source_target_pairs={{0,7},{1,0},{2,1},{3,2},{4,3},{5,4},{6,5},{7,6},{8,15},{9,8},{10,9... | collective-permute-start | bytes 393224 | tf_op jit(solution)/shard_map/ppermute | solution.py:216
  74.7 7.0 %copy-start.16 = (f32[1,64,512]{2,1,0:T(8,128)}, f32[1,64,512]{2,1,0:T(8,128)S(1)}, u32[]{:S(2)}) copy-start(f32[1,64,512]{2,1,0:T(8,128)S(1)} %collective-permute-done.10.refs_12_) | copy-start | bytes 393220
  74.7 7.0 %collective-permute-start.11 = (f32[1,64,512]{2,1,0:T(8,128)}, f32[1,64,512]{2,1,0:T(8,128)}, u32[]{:S(2)}, u32[]{:S(2)}) collective-permute-start(f32[1,64,512]{2,1,0:T(8,128)} %slice.30), channel_id=1, source_target_pairs={{0,1},{1,2},{2,3},{3,4},{4,5},{5,6},{6,7},{7,0},{8,9},{9,10},{10,1... | collective-permute-start | bytes 393224 | tf_op jit(solution)/shard_map/ppermute | solution.py:216
  81.7 11.6 %copy-start.2 = (s32[64,10]{0,1:T(8,128)S(1)}, s32[64,10]{0,1:T(8,128)}, u32[]{:S(2)}) copy-start(s32[64,10]{0,1:T(8,128)} %param.8) | copy-start | bytes 7684
  81.7 11.6 %copy-start.3 = (s32[64,4]{0,1:T(4,128)S(1)}, s32[64,4]{0,1:T(4,128)}, u32[]{:S(2)}) copy-start(s32[64,4]{0,1:T(4,128)} %param.7) | copy-start | bytes 3076
  81.7 11.6 %copy-start.4 = (s32[2]{0:T(128)S(1)}, s32[2]{0:T(128)}, u32[]{:S(2)}) copy-start(s32[2]{0:T(128)} %pad_add_fusion.pos.meta) | copy-start | bytes 28
  93.3 1.6 copy-start
  94.9 1.6 copy-start.1
  104.6 2.4 %collective-permute-start.19 = (f32[16,96,128]{2,1,0:T(8,128)S(1)}, f32[16,96,128]{2,1,0:T(8,128)S(1)}, u32[]{:S(2)}, u32[]{:S(2)}) collective-permute-start(f32[16,96,128]{2,1,0:T(8,128)S(1)} %get-tuple-element.16), channel_id=1, source_target_pairs={{0,8},{8,0},{16,24},{24,16},{32,40},{40,32},{48,56},{56,48},{64,72... | collective-permute-start | bytes 2359304 | tf_op jit(solution)/shard_map/ppermute | solution.py:219
  104.7 10.9 %collective-permute-start.12 = (f32[16,160,128]{2,1,0:T(8,128)}, f32[16,160,128]{2,1,0:T(8,128)S(1)}, u32[]{:S(2)}, u32[]{:S(2)}) collective-permute-start(f32[16,160,128]{2,1,0:T(8,128)} %get-tuple-element.12), channel_id=1, source_target_pairs={{0,8},{8,0},{16,24},{24,16},{32,40},{40,32},{48,56},{56,48},{64,72... | collective-permute-start | bytes 3932168 | tf_op jit(solution)/shard_map/ppermute | solution.py:219
  107.9 7.6 %copy-start.5 = (f32[16,160,128]{2,1,0:T(8,128)S(1)}, f32[16,160,128]{2,1,0:T(8,128)}, u32[]{:S(2)}) copy-start(f32[16,160,128]{2,1,0:T(8,128)} %get-tuple-element.11) | copy-start | bytes 3932164
  107.9 20.0 %all-to-all-start.1 = ((f32[16,96,128]{2,1,0:T(8,128)}), f32[16,96,128]{2,1,0:T(8,128)S(1)}, u32[]{:S(2)}, u32[]{:S(2)}) async-start(f32[16,96,128]{2,1,0:T(8,128)} %add.7), calls=%async_computation.1 | async-start | bytes 1572864 | tf_op jit(solution)/shard_map/all_to_all | solution.py:223
  127.9 23.3 %all-to-all-start = ((f32[16,160,128]{2,1,0:T(8,128)}), f32[16,160,128]{2,1,0:T(8,128)S(1)}, u32[]{:S(2)}, u32[]{:S(2)}) async-start(f32[16,160,128]{2,1,0:T(8,128)} %add.6), calls=%async_computation | async-start | bytes 2621440 | tf_op jit(solution)/shard_map/all_to_all | solution.py:223
  134.1 25.2 %copy-start.10 = (f32[96,128]{1,0:T(8,128)}, f32[96,128]{1,0:T(8,128)S(1)}, u32[]{:S(2)}) copy-start(f32[96,128]{1,0:T(8,128)S(1)} %reduce_sum.19.far) | copy-start | bytes 147460
  134.1 25.2 %collective-permute-start.20 = (f32[64,128]{1,0:T(8,128)S(1)}, f32[64,128]{1,0:T(8,128)S(1)}, u32[]{:S(2)}, u32[]{:S(2)}) collective-permute-start(f32[64,128]{1,0:T(8,128)S(1)} %slice.32), channel_id=1, source_target_pairs={{0,1},{1,2},{2,3},{3,4},{4,5},{5,6},{6,7},{7,0},{8,9},{9,10},{10,1... | collective-permute-start | bytes 98312 | tf_op jit(solution)/shard_map/ppermute | solution.py:216
  134.2 25.1 %collective-permute-start.21 = (f32[64,128]{1,0:T(8,128)S(1)}, f32[64,128]{1,0:T(8,128)S(1)}, u32[]{:S(2)}, u32[]{:S(2)}) collective-permute-start(f32[64,128]{1,0:T(8,128)S(1)} %slice.32), channel_id=1, source_target_pairs={{0,7},{1,0},{2,1},{3,2},{4,3},{5,4},{6,5},{7,6},{8,15},{9,8},{10,9... | collective-permute-start | bytes 98312 | tf_op jit(solution)/shard_map/ppermute | solution.py:216
  151.3 8.0 %copy-start.9 = (f32[160,128]{1,0:T(8,128)}, f32[160,128]{1,0:T(8,128)S(1)}, u32[]{:S(2)}) copy-start(f32[160,128]{1,0:T(8,128)S(1)} %reduce_sum.18.near) | copy-start | bytes 245764
  151.3 8.0 %collective-permute-start.13 = (f32[64,128]{1,0:T(8,128)S(1)}, f32[64,128]{1,0:T(8,128)S(1)}, u32[]{:S(2)}, u32[]{:S(2)}) collective-permute-start(f32[64,128]{1,0:T(8,128)S(1)} %slice.31), channel_id=1, source_target_pairs={{0,1},{1,2},{2,3},{3,4},{4,5},{5,6},{6,7},{7,0},{8,9},{9,10},{10,1... | collective-permute-start | bytes 98312 | tf_op jit(solution)/shard_map/ppermute | solution.py:216
  151.4 7.9 %collective-permute-start.14 = (f32[64,128]{1,0:T(8,128)S(1)}, f32[64,128]{1,0:T(8,128)S(1)}, u32[]{:S(2)}, u32[]{:S(2)}) collective-permute-start(f32[64,128]{1,0:T(8,128)S(1)} %slice.31), channel_id=1, source_target_pairs={{0,7},{1,0},{2,1},{3,2},{4,3},{5,4},{6,5},{7,6},{8,15},{9,8},{10,9... | collective-permute-start | bytes 98312 | tf_op jit(solution)/shard_map/ppermute | solution.py:216
  154.6 4.6 %collective-permute-start.22 = (f32[32,128]{1,0:T(8,128)S(1)}, f32[32,128]{1,0:T(8,128)S(1)}, u32[]{:S(2)}, u32[]{:S(2)}) collective-permute-start(f32[32,128]{1,0:T(8,128)S(1)} %slice.33), channel_id=1, source_target_pairs={{0,6},{1,7},{2,0},{3,1},{4,2},{5,3},{6,4},{7,5},{8,14},{9,15},{10,... | collective-permute-start | bytes 49160 | tf_op jit(solution)/shard_map/ppermute | solution.py:216
  159.2 0.6 copy-start.21
  159.2 0.6 copy-start.17
  159.3 0.6 copy-start.18
  159.3 0.6 copy-start.19
  159.9 0.6 copy-start.20
where the time goes:
time: 163 us; the launch traced here: 162 us
  waiting for transfers between devices  82.4 us (51%)
  starting transfers between devices  48.7 us (30%)
  Pallas kernels  21.3 us (13%)
  local copies, waits for them, and re-layouts  6.51 us (4%)
  other arithmetic  3 us (2%)
    ppermute x21, waiting for transfers between devices, along(): return lax.ppermute(x, 'narrow', [(i, (i + d) % 8) for i in range(8)])  55.7 us
    ppermute x21, starting transfers between devices, along(): return lax.ppermute(x, 'narrow', [(i, (i + d) % 8) for i in range(8)])  34.4 us
    all_to_all x2, waiting for transfers between devices, scatter(): return lax.all_to_all(x, 'wide', 0, 0, axis_index_groups=groups, tiled=True)  24.9 us
    all_to_all x2, starting transfers between devices, scatter(): return lax.all_to_all(x, 'wide', 0, 0, axis_index_groups=groups, tiled=True)  13.7 us
    pallas_call x1, Pallas kernels, level(): near(*scalars, panels, *u1, *d1, factors, fu[1], fd[1], fu[2], fd[2], fu[...  11.5 us
    pallas_call x1, Pallas kernels, level(): keep2, send2 = far(*scalars, *u2, *d2, f3, n3)  8.05 us
    unnamed x44, local copies, waits for them, and re-layouts  4.41 us
  transfers between devices with their start and end apart: 25, of which 11 were waited for; matrix products, arithmetic and copies ran while one was open for 2% of the time, Pallas kernels for 7%

commit v1 on v0

--- a/solution.py
+++ b/solution.py
@@ -7,9 +7,16 @@
 
 
 PAIRS = tuple((k, l) for k in range(4) for l in range(k + 1))
-BOUNDS = (0, 4, 8)
-CHUNKS = len(BOUNDS) - 1
-SPOTS = tuple((c, b - BOUNDS[c]) for c in range(CHUNKS) for b in range(BOUNDS[c], BOUNDS[c + 1]))
+BOUNDS = (0, 2, 4, 8)
+FAR_BOUNDS = (0, 4, 8)
+CHUNKS, FAR_CHUNKS = len(BOUNDS) - 1, len(FAR_BOUNDS) - 1
+
+
+def spots(bounds):
+    return tuple((c, b - bounds[c]) for c in range(len(bounds) - 1) for b in range(bounds[c], bounds[c + 1]))
+
+
+SPOTS, FAR_SPOTS = spots(BOUNDS), spots(FAR_BOUNDS)
 ANY = pl.BlockSpec(memory_space=pltpu.HBM)
 SMEM = pl.BlockSpec(memory_space=pltpu.SMEM)
 VMEM = pl.BlockSpec(memory_space=pltpu.VMEM)
@@ -132,10 +139,10 @@
 def far_kernel(pos, member, target, *refs):
     *refs, meta = refs
     prepare(pos, member, target, meta)
-    up, down = refs[:CHUNKS], refs[CHUNKS : 2 * CHUNKS]
-    f_in, n_in = refs[2 * CHUNKS : 2 + 2 * CHUNKS]
-    keep, send = refs[2 + 2 * CHUNKS : 4 + 2 * CHUNKS]
-    x, f3, near, left, right, prod, acc, isem, xsem, osem = refs[4 + 2 * CHUNKS :]
+    up, down = refs[:FAR_CHUNKS], refs[FAR_CHUNKS : 2 * FAR_CHUNKS]
+    f_in, n_in = refs[2 * FAR_CHUNKS : 2 + 2 * FAR_CHUNKS]
+    keep, send = refs[2 + 2 * FAR_CHUNKS : 4 + 2 * FAR_CHUNKS]
+    x, f3, near, left, right, prod, acc, isem, xsem, osem = refs[4 + 2 * FAR_CHUNKS :]
     copies = []
     ins = (
         (f_in, f3.at[:, pl.ds(0, 1024)]),
@@ -150,7 +157,7 @@
         c.start()
     for piece in range(2):
         for b in range(8):
-            src = (up, down)[piece][SPOTS[b][0]].at[SPOTS[b][1]]
+            src = (up, down)[piece][FAR_SPOTS[b][0]].at[FAR_SPOTS[b][1]]
             c = pltpu.make_async_copy(src, x.at[piece, meta[2 + b]], xsem.at[piece * 8 + b])
             c.start()
             xcopies.append(c)
@@ -231,8 +238,13 @@
     fd4 = along(fd[3][1:], -1)
     u1 = [along(c, 1) for c in chunks]
     d1 = [along(c, -1) for c in chunks]
-    u2 = [along(c, 1) for c in u1]
-    d2 = [along(c, -1) for c in d1]
+
+    def joined(pieces, c):
+        parts = [p for p, low, high in zip(pieces, BOUNDS, BOUNDS[1:]) if FAR_BOUNDS[c] <= low and high <= FAR_BOUNDS[c + 1]]
+        return parts[0] if len(parts) == 1 else jnp.concatenate(parts)
+
+    u2 = [along(joined(u1, c), 1) for c in range(FAR_CHUNKS)]
+    d2 = [along(joined(d1, c), -1) for c in range(FAR_CHUNKS)]
 
     early = jax.ShapeDtypeStruct((16, 160, 128), F32)
     late = jax.ShapeDtypeStruct((16, 96, 128), F32)
@@ -268,7 +280,7 @@
         name="far",
         compiler_params=pltpu.CompilerParams(vmem_limit_bytes=24 << 20),
         out_shape=(late, late),
-        in_specs=[SMEM] * 3 + [ANY] * (2 + 2 * CHUNKS),
+        in_specs=[SMEM] * 3 + [ANY] * (2 + 2 * FAR_CHUNKS),
         out_specs=(ANY,) * 2,
         scratch_shapes=[
             pltpu.VMEM((2, 8, 64, 512), F32),
@@ -291,6 +303,7 @@
     return pl.pallas_call(
         final_kernel,
         name="final",
+        compiler_params=pltpu.CompilerParams(vmem_limit_bytes=4 << 20),
         out_shape=jax.ShapeDtypeStruct((1, 64, 512), F32),
         in_specs=[SMEM] + [VMEM] * 8,
         out_specs=VMEM,

time: 163 us -> 159 us (0.975)
  starting transfers between devices: 48.7 us -> 43.9 us
  other arithmetic: 3 us -> 5.93 us
    ppermute x21 -> x23, starting transfers between devices: 34.4 us -> 29.6 us  [along(): return lax.ppermute(x, 'narrow', [(i, (i + d) % 8) for i in range(8)])]
    concatenate x0 -> x2, other arithmetic: none -> 1.73 us  [joined(): return parts[0] if len(parts) == 1 else jnp.concatenate(parts)]
    unnamed x44 -> x40, local copies, waits for them, and re-layouts: 4.41 us -> 3.87 us
    ppermute x21 -> x23, waiting for transfers between devices: 55.7 us -> 55.9 us  [along(): return lax.ppermute(x, 'narrow', [(i, (i + d) % 8) for i in range(8)])]
  transfers between devices with their start and end apart: 25 -> 27, of which waited for: 11 -> 14; matrix products, arithmetic and copies ran while one was open for 2% -> 5% of each run, Pallas kernels for 7% -> 7%
where the time goes in v1:
time: 159 us; the launch traced here: 158 us
  waiting for transfers between devices  81.1 us (51%)
  starting transfers between devices  43.9 us (28%)
  Pallas kernels  21 us (13%)
  other arithmetic  5.93 us (4%)
  local copies, waits for them, and re-layouts  5.65 us (4%)
    ppermute x23, waiting for transfers between devices, along(): return lax.ppermute(x, 'narrow', [(i, (i + d) % 8) for i in range(8)])  55.9 us
    ppermute x23, starting transfers between devices, along(): return lax.ppermute(x, 'narrow', [(i, (i + d) % 8) for i in range(8)])  29.6 us
    all_to_all x2, waiting for transfers between devices, scatter(): return lax.all_to_all(x, 'wide', 0, 0, axis_index_groups=groups, tiled=True)  23.4 us
    all_to_all x2, starting transfers between devices, scatter(): return lax.all_to_all(x, 'wide', 0, 0, axis_index_groups=groups, tiled=True)  13.7 us
    pallas_call x1, Pallas kernels, level(): near(*scalars, panels, *u1, *d1, factors, fu[1], fd[1], fu[2], fd[2], fu[...  11.6 us
    pallas_call x1, Pallas kernels, level(): keep2, send2 = far(*scalars, *u2, *d2, f3, n3)  8.05 us
    unnamed x40, local copies, waits for them, and re-layouts  3.87 us
  transfers between devices with their start and end apart: 27, of which 14 were waited for; matrix products, arithmetic and copies ran while one was open for 5% of the time, Pallas kernels for 7%

profile of v1, /device:TPU:2, one launch (start us, length us, event | category | flops | bytes accessed | tf_op | source)
XLA Modules:
  0.0 157.8 jit_solution(11308274341691916940)
XLA Ops:
  0.0 5.9 %collective-permute-start.7 = (f32[2,64,512]{2,1,0:T(8,128)}, f32[2,64,512]{2,1,0:T(8,128)S(1)}, u32[]{:S(2)}, u32[]{:S(2)}) collective-permute-start(f32[2,64,512]{2,1,0:T(8,128)} %refs_7_.1), channel_id=1, source_target_pairs={{0,7},{1,0},{2,1},{3,2},{4,3},{5,4},{6,5},{7,6},{8,15},{9,8},{10,9... | collective-permute-start | bytes 786440 | tf_op jit(solution)/shard_map/ppermute | solution.py:223
  5.9 0.0 collective-permute-start.6
  5.9 1.1 fusion
  6.9 0.1 collective-permute-start
  7.0 0.1 collective-permute-start.1
  7.1 3.3 %collective-permute-start.3 = (f32[2,64,512]{2,1,0:T(8,128)S(1)}, f32[2,64,512]{2,1,0:T(8,128)S(1)}, u32[]{:S(2)}, u32[]{:S(2)}) collective-permute-start(f32[2,64,512]{2,1,0:T(8,128)S(1)} %get-tuple-element.18), channel_id=1, source_target_pairs={{0,7},{1,0},{2,1},{3,2},{4,3},{5,4},{6,5},{7,6},{8,15},{9,8},{10,9... | collective-permute-start | bytes 786440 | tf_op jit(solution)/shard_map/ppermute | solution.py:223
  10.5 2.4 %collective-permute-done.7.refs_9_ = f32[2,64,512]{2,1,0:T(8,128)S(1)} collective-permute-done((f32[2,64,512]{2,1,0:T(8,128)}, f32[2,64,512]{2,1,0:T(8,128)S(1)}, u32[]{:S(2)}, u32[]{:S(2)}) %collective-permute-start.7) | collective-permute-done | bytes 262176 | tf_op jit(solution)/shard_map/ppermute | solution.py:223
  12.9 0.0 collective-permute-start.2
  12.9 3.6 %collective-permute-done.6.refs_8_ = f32[2,64,512]{2,1,0:T(8,128)S(1)} collective-permute-done((f32[2,64,512]{2,1,0:T(8,128)}, f32[2,64,512]{2,1,0:T(8,128)S(1)}, u32[]{:S(2)}, u32[]{:S(2)}) %collective-permute-start.6) | collective-permute-done | bytes 262176 | tf_op jit(solution)/shard_map/ppermute | solution.py:223
  16.5 0.1 collective-permute-start.5
  16.6 5.5 %collective-permute-done.refs_1_ = f32[2,64,512]{2,1,0:T(8,128)S(1)} collective-permute-done((f32[2,64,512]{2,1,0:T(8,128)S(1)}, f32[2,64,512]{2,1,0:T(8,128)S(1)}, u32[]{:S(2)}, u32[]{:S(2)}) %collective-permute-start) | collective-permute-done | bytes 262176 | tf_op jit(solution)/shard_map/ppermute | solution.py:223
  22.1 0.0 collective-permute-start.9
  22.1 5.6 %collective-permute-done.1.refs_2_ = f32[2,64,512]{2,1,0:T(8,128)S(1)} collective-permute-done((f32[2,64,512]{2,1,0:T(8,128)S(1)}, f32[2,64,512]{2,1,0:T(8,128)S(1)}, u32[]{:S(2)}, u32[]{:S(2)}) %collective-permute-start.1) | collective-permute-done | bytes 262176 | tf_op jit(solution)/shard_map/ppermute | solution.py:223
  27.7 0.0 collective-permute-start.4
  27.7 0.0 collective-permute-done.3.refs_4_
  27.7 2.0 %collective-permute-start.8 = (f32[2,64,512]{2,1,0:T(8,128)S(1)}, f32[2,64,512]{2,1,0:T(8,128)S(1)}, u32[]{:S(2)}, u32[]{:S(2)}) collective-permute-start(f32[2,64,512]{2,1,0:T(8,128)S(1)} %collective-permute-done.6.refs_8_), channel_id=1, source_target_pairs={{0,1},{1,2},{2,3},{3,4},{4,5},{5,6},{6,7},{7,0},{8,9},{9,10},{10,1... | collective-permute-start | bytes 786440 | tf_op jit(solution)/shard_map/ppermute | solution.py:223
  29.7 6.6 %collective-permute-done.9.refs_11_ = f32[2,64,512]{2,1,0:T(8,128)S(1)} collective-permute-done((f32[2,64,512]{2,1,0:T(8,128)S(1)}, f32[2,64,512]{2,1,0:T(8,128)S(1)}, u32[]{:S(2)}, u32[]{:S(2)}) %collective-permute-start.9) | collective-permute-done | bytes 262176 | tf_op jit(solution)/shard_map/ppermute | solution.py:223
  36.3 2.6 %collective-permute-start.11 = (f32[2,64,512]{2,1,0:T(8,128)S(1)}, f32[2,64,512]{2,1,0:T(8,128)S(1)}, u32[]{:S(2)}, u32[]{:S(2)}) collective-permute-start(f32[2,64,512]{2,1,0:T(8,128)S(1)} %collective-permute-done.9.refs_11_), channel_id=1, source_target_pairs={{0,7},{1,0},{2,1},{3,2},{4,3},{5,4},{6,5},{7,6},{8,15},{9,8},{10,9... | collective-permute-start | bytes 786440 | tf_op jit(solution)/shard_map/ppermute | solution.py:223
  38.9 0.9 pad_maximum_fusion
  39.8 1.8 %collective-permute-done.4.refs_5_ = f32[2,64,512]{2,1,0:T(8,128)S(1)} collective-permute-done((f32[2,64,512]{2,1,0:T(8,128)S(1)}, f32[2,64,512]{2,1,0:T(8,128)S(1)}, u32[]{:S(2)}, u32[]{:S(2)}) %collective-permute-start.4) | collective-permute-done | bytes 262176 | tf_op jit(solution)/shard_map/ppermute | solution.py:223
  41.6 0.0 collective-permute-start.17
  41.6 1.5 collective-permute-done.8.refs_10_
  43.1 0.4 collective-permute-start.10
  43.6 0.9 pad_maximum_fusion.1
  44.5 0.0 collective-permute-done.2.refs_3_
  44.5 2.9 %collective-permute-start.19 = (f32[4,64,512]{2,1,0:T(8,128)}, f32[4,64,512]{2,1,0:T(8,128)S(1)}, u32[]{:S(2)}, u32[]{:S(2)}) collective-permute-start(f32[4,64,512]{2,1,0:T(8,128)} %pad_maximum_fusion.1), channel_id=1, source_target_pairs={{0,7},{1,0},{2,1},{3,2},{4,3},{5,4},{6,5},{7,6},{8,15},{9,8},{10,9... | collective-permute-start | bytes 1572872 | tf_op jit(solution)/shard_map/ppermute | solution.py:223
  47.3 0.0 collective-permute-done.5.refs_6_
  47.3 0.0 collective-permute-start.18
  47.3 0.0 collective-permute-done.11.refs_13_
  47.4 3.5 %collective-permute-start.20 = (f32[4,64,512]{2,1,0:T(8,128)}, f32[4,64,512]{2,1,0:T(8,128)S(1)}, u32[]{:S(2)}, u32[]{:S(2)}) collective-permute-start(f32[4,64,512]{2,1,0:T(8,128)} %collective-permute-done.5.refs_6_), channel_id=1, source_target_pairs={{0,7},{1,0},{2,1},{3,2},{4,3},{5,4},{6,5},{7,6},{8,15},{9,8},{10,9... | collective-permute-start | bytes 1572872 | tf_op jit(solution)/shard_map/ppermute | solution.py:223
  50.9 12.6 %collective-permute-done.10.refs_12_ = f32[2,64,512]{2,1,0:T(8,128)S(1)} collective-permute-done((f32[2,64,512]{2,1,0:T(8,128)S(1)}, f32[2,64,512]{2,1,0:T(8,128)S(1)}, u32[]{:S(2)}, u32[]{:S(2)}) %collective-permute-start.10) | collective-permute-done | bytes 262176 | tf_op jit(solution)/shard_map/ppermute | solution.py:223
  63.5 1.7 %collective-permute-start.12 = (f32[1,64,512]{2,1,0:T(8,128)S(1)}, f32[1,64,512]{2,1,0:T(8,128)S(1)}, u32[]{:S(2)}, u32[]{:S(2)}) collective-permute-start(f32[1,64,512]{2,1,0:T(8,128)S(1)} %slice.33), channel_id=1, source_target_pairs={{0,7},{1,0},{2,1},{3,2},{4,3},{5,4},{6,5},{7,6},{8,15},{9,8},{10,9... | collective-permute-start | bytes 393224 | tf_op jit(solution)/shard_map/ppermute | solution.py:223
  65.2 0.7 slice.34
  65.8 5.5 %collective-permute-done.12.refs_14_ = f32[1,64,512]{2,1,0:T(8,128)S(1)} collective-permute-done((f32[1,64,512]{2,1,0:T(8,128)S(1)}, f32[1,64,512]{2,1,0:T(8,128)S(1)}, u32[]{:S(2)}, u32[]{:S(2)}) %collective-permute-start.12) | collective-permute-done | bytes 131104 | tf_op jit(solution)/shard_map/ppermute | solution.py:223
  71.4 0.0 collective-permute-start.13
  71.4 0.6 pad_add_fusion.pos.meta
  71.9 6.3 %collective-permute-done.13.refs_15_ = f32[1,64,512]{2,1,0:T(8,128)S(1)} collective-permute-done((f32[1,64,512]{2,1,0:T(8,128)}, f32[1,64,512]{2,1,0:T(8,128)S(1)}, u32[]{:S(2)}, u32[]{:S(2)}) %collective-permute-start.13) | collective-permute-done | bytes 131104 | tf_op jit(solution)/shard_map/ppermute | solution.py:223
  78.2 0.6 copy-done.19
  78.9 11.6 %near.1 = (f32[16,160,128]{2,1,0:T(8,128)}, f32[16,160,128]{2,1,0:T(8,128)}, bf16[2,1024,512]{2,1,0:T(8,128)(2,1)}, bf16[2,2,256,1024]{3,2,1,0:T(8,128)(2,1)}) custom-call(s32[2]{0:T(128)} %pad_add_fusion.pos.meta, s32[4,64]{1,0:T(4,128)} %bitcast.6, s32[10,64]{1,0:T(8,128)} %bitcast.4, f32[8,64,512]{2,1,0:T(8,128)} %refs_0_.1, f32[2,64,512]{2,1,0:T(8,128)} %copy-done.8, ...), custom_call_target="tpu_custom_call" | custom-call | tf_op jit(solution)/shard_map/near/pallas_call | solution.py:274
  90.5 0.0 collective-permute-done.17.refs_0_
  90.5 0.0 collective-permute-done.19.refs_2_
  90.6 1.6 %copy-done = bf16[2,1024,512]{2,1,0:T(8,128)(2,1)S(1)} copy-done((bf16[2,1024,512]{2,1,0:T(8,128)(2,1)S(1)}, bf16[2,1024,512]{2,1,0:T(8,128)(2,1)}, u32[]{:S(2)}) %copy-start) | copy-done | bytes 2097176
  92.2 1.6 %copy-done.1 = bf16[2,2,256,1024]{3,2,1,0:T(8,128)(2,1)S(1)} copy-done((bf16[2,2,256,1024]{3,2,1,0:T(8,128)(2,1)S(1)}, bf16[2,2,256,1024]{3,2,1,0:T(8,128)(2,1)}, u32[]{:S(2)}) %copy-start.1) | copy-done | bytes 2097176
  93.7 8.1 %far.1 = (f32[16,96,128]{2,1,0:T(8,128)S(1)}, f32[16,96,128]{2,1,0:T(8,128)S(1)}) custom-call(s32[2]{0:T(128)S(1)} %copy-done.5, s32[4,64]{1,0:T(4,128)S(1)} %bitcast.7, s32[10,64]{1,0:T(8,128)S(1)} %bitcast.5, f32[4,64,512]{2,1,0:T(8,128)S(1)} %collective-permute-done.17.refs_0_, f32[4,64,512]{2,1,0:T(8,128)S(1)} %collective-permute-done.18.refs_1_, ...), custom_call_target="tpu_custom_call" | custom-call | tf_op jit(solution)/shard_map/far/pallas_call | solution.py:299
  101.8 0.1 collective-permute-start.21
  101.9 0.5 collective-permute-start.14
  102.4 1.8 %collective-permute-done.21 = f32[16,96,128]{2,1,0:T(8,128)S(1)} collective-permute-done((f32[16,96,128]{2,1,0:T(8,128)S(1)}, f32[16,96,128]{2,1,0:T(8,128)S(1)}, u32[]{:S(2)}, u32[]{:S(2)}) %collective-permute-start.21) | collective-permute-done | bytes 786464 | tf_op jit(solution)/shard_map/ppermute | solution.py:226
  104.2 1.0 add.7
  105.2 7.6 %all-to-all-start.1 = ((f32[16,96,128]{2,1,0:T(8,128)}), f32[16,96,128]{2,1,0:T(8,128)S(1)}, u32[]{:S(2)}, u32[]{:S(2)}) async-start(f32[16,96,128]{2,1,0:T(8,128)} %add.7), calls=%async_computation.1 | async-start | bytes 1572864 | tf_op jit(solution)/shard_map/all_to_all | solution.py:230
  112.8 2.5 %add.6 = f32[16,160,128]{2,1,0:T(8,128)} add(f32[16,160,128]{2,1,0:T(8,128)S(1)} %copy-done.7, f32[16,160,128]{2,1,0:T(8,128)} %collective-permute-done.14) | non-fusion elementwise | flops 327680 | bytes 3932160 | tf_op jit(solution)/shard_map/add | solution.py:275
  115.3 9.8 %all-to-all-done.1 = f32[16,96,128]{2,1,0:T(8,128)S(1)} async-done(((f32[16,96,128]{2,1,0:T(8,128)}), f32[16,96,128]{2,1,0:T(8,128)S(1)}, u32[]{:S(2)}, u32[]{:S(2)}) %all-to-all-start.1) | async-done | bytes 786464 | tf_op jit(solution)/shard_map/all_to_all | solution.py:230
  125.2 6.1 %all-to-all-start = ((f32[16,160,128]{2,1,0:T(8,128)}), f32[16,160,128]{2,1,0:T(8,128)S(1)}, u32[]{:S(2)}, u32[]{:S(2)}) async-start(f32[16,160,128]{2,1,0:T(8,128)} %add.6), calls=%async_computation | async-start | bytes 2621440 | tf_op jit(solution)/shard_map/all_to_all | solution.py:230
  131.3 0.3 collective-permute-start.22
  131.6 3.2 %collective-permute-start.23 = (f32[64,128]{1,0:T(8,128)S(1)}, f32[64,128]{1,0:T(8,128)S(1)}, u32[]{:S(2)}, u32[]{:S(2)}) collective-permute-start(f32[64,128]{1,0:T(8,128)S(1)} %slice.36), channel_id=1, source_target_pairs={{0,7},{1,0},{2,1},{3,2},{4,3},{5,4},{6,5},{7,6},{8,15},{9,8},{10,9... | collective-permute-start | bytes 98312 | tf_op jit(solution)/shard_map/ppermute | solution.py:223
  134.9 13.6 %all-to-all-done = f32[16,160,128]{2,1,0:T(8,128)S(1)} async-done(((f32[16,160,128]{2,1,0:T(8,128)}), f32[16,160,128]{2,1,0:T(8,128)S(1)}, u32[]{:S(2)}, u32[]{:S(2)}) %all-to-all-start) | async-done | bytes 1310752 | tf_op jit(solution)/shard_map/all_to_all | solution.py:230
  148.4 0.1 reduce_sum.18.near
  148.5 0.1 collective-permute-start.15
  148.6 3.2 %collective-permute-start.16 = (f32[64,128]{1,0:T(8,128)S(1)}, f32[64,128]{1,0:T(8,128)S(1)}, u32[]{:S(2)}, u32[]{:S(2)}) collective-permute-start(f32[64,128]{1,0:T(8,128)S(1)} %slice.35), channel_id=1, source_target_pairs={{0,7},{1,0},{2,1},{3,2},{4,3},{5,4},{6,5},{7,6},{8,15},{9,8},{10,9... | collective-permute-start | bytes 98312 | tf_op jit(solution)/shard_map/ppermute | solution.py:223
  151.8 0.2 collective-permute-start.24
  152.1 4.4 %collective-permute-done.24.cd = f32[32,128]{1,0:T(8,128)S(1)} collective-permute-done((f32[32,128]{1,0:T(8,128)S(1)}, f32[32,128]{1,0:T(8,128)S(1)}, u32[]{:S(2)}, u32[]{:S(2)}) %collective-permute-start.24) | collective-permute-done | bytes 16416 | tf_op jit(solution)/shard_map/ppermute | solution.py:223
  156.5 0.0 collective-permute-done.23.dd
  156.5 0.0 collective-permute-done.15.eu
  156.5 0.0 collective-permute-done.16.ed
  156.5 1.3 final.1
  (47 shorter events, 0.2 us)
Async XLA Ops:
  0.0 10.4 %copy-start.6 = (f32[8,64,512]{2,1,0:T(8,128)S(1)}, f32[8,64,512]{2,1,0:T(8,128)}, u32[]{:S(2)}) copy-start(f32[8,64,512]{2,1,0:T(8,128)} %refs_0_.1) | copy-start | bytes 3145732
  0.0 12.9 %collective-permute-start.7 = (f32[2,64,512]{2,1,0:T(8,128)}, f32[2,64,512]{2,1,0:T(8,128)S(1)}, u32[]{:S(2)}, u32[]{:S(2)}) collective-permute-start(f32[2,64,512]{2,1,0:T(8,128)} %refs_7_.1), channel_id=1, source_target_pairs={{0,7},{1,0},{2,1},{3,2},{4,3},{5,4},{6,5},{7,6},{8,15},{9,8},{10,9... | collective-permute-start | bytes 786440 | tf_op jit(solution)/shard_map/ppermute | solution.py:223
  5.9 10.6 %collective-permute-start.6 = (f32[2,64,512]{2,1,0:T(8,128)}, f32[2,64,512]{2,1,0:T(8,128)S(1)}, u32[]{:S(2)}, u32[]{:S(2)}) collective-permute-start(f32[2,64,512]{2,1,0:T(8,128)} %refs_7_.1), channel_id=1, source_target_pairs={{0,1},{1,2},{2,3},{3,4},{4,5},{5,6},{6,7},{7,0},{8,9},{9,10},{10,1... | collective-permute-start | bytes 786440 | tf_op jit(solution)/shard_map/ppermute | solution.py:223
  6.9 15.1 %collective-permute-start = (f32[2,64,512]{2,1,0:T(8,128)S(1)}, f32[2,64,512]{2,1,0:T(8,128)S(1)}, u32[]{:S(2)}, u32[]{:S(2)}) collective-permute-start(f32[2,64,512]{2,1,0:T(8,128)S(1)} %get-tuple-element.18), channel_id=1, source_target_pairs={{0,1},{1,2},{2,3},{3,4},{4,5},{5,6},{6,7},{7,0},{8,9},{9,10},{10,1... | collective-permute-start | bytes 786440 | tf_op jit(solution)/shard_map/ppermute | solution.py:223
  7.0 20.7 %collective-permute-start.1 = (f32[2,64,512]{2,1,0:T(8,128)S(1)}, f32[2,64,512]{2,1,0:T(8,128)S(1)}, u32[]{:S(2)}, u32[]{:S(2)}) collective-permute-start(f32[2,64,512]{2,1,0:T(8,128)S(1)} %get-tuple-element.17), channel_id=1, source_target_pairs={{0,1},{1,2},{2,3},{3,4},{4,5},{5,6},{6,7},{7,0},{8,9},{9,10},{10,1... | collective-permute-start | bytes 786440 | tf_op jit(solution)/shard_map/ppermute | solution.py:223
  7.1 20.6 %collective-permute-start.3 = (f32[2,64,512]{2,1,0:T(8,128)S(1)}, f32[2,64,512]{2,1,0:T(8,128)S(1)}, u32[]{:S(2)}, u32[]{:S(2)}) collective-permute-start(f32[2,64,512]{2,1,0:T(8,128)S(1)} %get-tuple-element.18), channel_id=1, source_target_pairs={{0,7},{1,0},{2,1},{3,2},{4,3},{5,4},{6,5},{7,6},{8,15},{9,8},{10,9... | collective-permute-start | bytes 786440 | tf_op jit(solution)/shard_map/ppermute | solution.py:223
  12.9 31.6 %copy-start.14 = (f32[2,64,512]{2,1,0:T(8,128)}, f32[2,64,512]{2,1,0:T(8,128)S(1)}, u32[]{:S(2)}) copy-start(f32[2,64,512]{2,1,0:T(8,128)S(1)} %collective-permute-done.7.refs_9_) | copy-start | bytes 786436
  12.9 31.6 %collective-permute-start.2 = (f32[4,64,512]{2,1,0:T(8,128)S(1)}, f32[4,64,512]{2,1,0:T(8,128)}, u32[]{:S(2)}, u32[]{:S(2)}) collective-permute-start(f32[4,64,512]{2,1,0:T(8,128)S(1)} %slice.27), channel_id=1, source_target_pairs={{0,1},{1,2},{2,3},{3,4},{4,5},{5,6},{6,7},{7,0},{8,9},{9,10},{10,1... | collective-permute-start | bytes 1572872 | tf_op jit(solution)/shard_map/ppermute | solution.py:223
  16.5 30.9 %copy-start.15 = (f32[2,64,512]{2,1,0:T(8,128)}, f32[2,64,512]{2,1,0:T(8,128)S(1)}, u32[]{:S(2)}) copy-start(f32[2,64,512]{2,1,0:T(8,128)S(1)} %collective-permute-done.6.refs_8_) | copy-start | bytes 786436
  16.5 30.9 %collective-permute-start.5 = (f32[4,64,512]{2,1,0:T(8,128)S(1)}, f32[4,64,512]{2,1,0:T(8,128)}, u32[]{:S(2)}, u32[]{:S(2)}) collective-permute-start(f32[4,64,512]{2,1,0:T(8,128)S(1)} %slice.27), channel_id=1, source_target_pairs={{0,7},{1,0},{2,1},{3,2},{4,3},{5,4},{6,5},{7,6},{8,15},{9,8},{10,9... | collective-permute-start | bytes 1572872 | tf_op jit(solution)/shard_map/ppermute | solution.py:223
  22.1 43.8 %copy-start.8 = (f32[2,64,512]{2,1,0:T(8,128)}, f32[2,64,512]{2,1,0:T(8,128)S(1)}, u32[]{:S(2)}) copy-start(f32[2,64,512]{2,1,0:T(8,128)S(1)} %collective-permute-done.refs_1_) | copy-start | bytes 786436
  22.1 14.2 %collective-permute-start.9 = (f32[2,64,512]{2,1,0:T(8,128)S(1)}, f32[2,64,512]{2,1,0:T(8,128)S(1)}, u32[]{:S(2)}, u32[]{:S(2)}) collective-permute-start(f32[2,64,512]{2,1,0:T(8,128)S(1)} %collective-permute-done.7.refs_9_), channel_id=1, source_target_pairs={{0,7},{1,0},{2,1},{3,2},{4,3},{5,4},{6,5},{7,6},{8,15},{9,8},{10,9... | collective-permute-start | bytes 786440 | tf_op jit(solution)/shard_map/ppermute | solution.py:223
  27.7 38.1 %copy-start.9 = (f32[2,64,512]{2,1,0:T(8,128)}, f32[2,64,512]{2,1,0:T(8,128)S(1)}, u32[]{:S(2)}) copy-start(f32[2,64,512]{2,1,0:T(8,128)S(1)} %collective-permute-done.1.refs_2_) | copy-start | bytes 786436
  27.7 13.9 %collective-permute-start.4 = (f32[2,64,512]{2,1,0:T(8,128)S(1)}, f32[2,64,512]{2,1,0:T(8,128)S(1)}, u32[]{:S(2)}, u32[]{:S(2)}) collective-permute-start(f32[2,64,512]{2,1,0:T(8,128)S(1)} %get-tuple-element.17), channel_id=1, source_target_pairs={{0,7},{1,0},{2,1},{3,2},{4,3},{5,4},{6,5},{7,6},{8,15},{9,8},{10,9... | collective-permute-start | bytes 786440 | tf_op jit(solution)/shard_map/ppermute | solution.py:223
  27.7 16.7 %copy-start.10 = (f32[2,64,512]{2,1,0:T(8,128)}, f32[2,64,512]{2,1,0:T(8,128)S(1)}, u32[]{:S(2)}) copy-start(f32[2,64,512]{2,1,0:T(8,128)S(1)} %collective-permute-done.3.refs_4_) | copy-start | bytes 786436
  27.7 15.4 %collective-permute-start.8 = (f32[2,64,512]{2,1,0:T(8,128)S(1)}, f32[2,64,512]{2,1,0:T(8,128)S(1)}, u32[]{:S(2)}, u32[]{:S(2)}) collective-permute-start(f32[2,64,512]{2,1,0:T(8,128)S(1)} %collective-permute-done.6.refs_8_), channel_id=1, source_target_pairs={{0,1},{1,2},{2,3},{3,4},{4,5},{5,6},{6,7},{7,0},{8,9},{9,10},{10,1... | collective-permute-start | bytes 786440 | tf_op jit(solution)/shard_map/ppermute | solution.py:223
  36.3 29.5 %copy-start.16 = (f32[2,64,512]{2,1,0:T(8,128)}, f32[2,64,512]{2,1,0:T(8,128)S(1)}, u32[]{:S(2)}) copy-start(f32[2,64,512]{2,1,0:T(8,128)S(1)} %collective-permute-done.9.refs_11_) | copy-start | bytes 786436
  36.3 11.0 %collective-permute-start.11 = (f32[2,64,512]{2,1,0:T(8,128)S(1)}, f32[2,64,512]{2,1,0:T(8,128)S(1)}, u32[]{:S(2)}, u32[]{:S(2)}) collective-permute-start(f32[2,64,512]{2,1,0:T(8,128)S(1)} %collective-permute-done.9.refs_11_), channel_id=1, source_target_pairs={{0,7},{1,0},{2,1},{3,2},{4,3},{5,4},{6,5},{7,6},{8,15},{9,8},{10,9... | collective-permute-start | bytes 786440 | tf_op jit(solution)/shard_map/ppermute | solution.py:223
  41.6 36.6 %copy-start.11 = (f32[2,64,512]{2,1,0:T(8,128)}, f32[2,64,512]{2,1,0:T(8,128)S(1)}, u32[]{:S(2)}) copy-start(f32[2,64,512]{2,1,0:T(8,128)S(1)} %collective-permute-done.4.refs_5_) | copy-start | bytes 786436
  41.6 48.9 %collective-permute-start.17 = (f32[4,64,512]{2,1,0:T(8,128)}, f32[4,64,512]{2,1,0:T(8,128)S(1)}, u32[]{:S(2)}, u32[]{:S(2)}) collective-permute-start(f32[4,64,512]{2,1,0:T(8,128)} %pad_maximum_fusion), channel_id=1, source_target_pairs={{0,1},{1,2},{2,3},{3,4},{4,5},{5,6},{6,7},{7,0},{8,9},{9,10},{10,1... | collective-permute-start | bytes 1572872 | tf_op jit(solution)/shard_map/ppermute | solution.py:223
  43.1 28.2 %copy-start.17 = (f32[2,64,512]{2,1,0:T(8,128)}, f32[2,64,512]{2,1,0:T(8,128)S(1)}, u32[]{:S(2)}) copy-start(f32[2,64,512]{2,1,0:T(8,128)S(1)} %collective-permute-done.8.refs_10_) | copy-start | bytes 786436
  43.1 20.3 %collective-permute-start.10 = (f32[2,64,512]{2,1,0:T(8,128)S(1)}, f32[2,64,512]{2,1,0:T(8,128)S(1)}, u32[]{:S(2)}, u32[]{:S(2)}) collective-permute-start(f32[2,64,512]{2,1,0:T(8,128)S(1)} %collective-permute-done.8.refs_10_), channel_id=1, source_target_pairs={{0,1},{1,2},{2,3},{3,4},{4,5},{5,6},{6,7},{7,0},{8,9},{9,10},{10,1... | collective-permute-start | bytes 786440 | tf_op jit(solution)/shard_map/ppermute | solution.py:223
  44.5 46.0 %collective-permute-start.19 = (f32[4,64,512]{2,1,0:T(8,128)}, f32[4,64,512]{2,1,0:T(8,128)S(1)}, u32[]{:S(2)}, u32[]{:S(2)}) collective-permute-start(f32[4,64,512]{2,1,0:T(8,128)} %pad_maximum_fusion.1), channel_id=1, source_target_pairs={{0,7},{1,0},{2,1},{3,2},{4,3},{5,4},{6,5},{7,6},{8,15},{9,8},{10,9... | collective-permute-start | bytes 1572872 | tf_op jit(solution)/shard_map/ppermute | solution.py:223
  47.3 43.2 %collective-permute-start.18 = (f32[4,64,512]{2,1,0:T(8,128)}, f32[4,64,512]{2,1,0:T(8,128)S(1)}, u32[]{:S(2)}, u32[]{:S(2)}) collective-permute-start(f32[4,64,512]{2,1,0:T(8,128)} %collective-permute-done.2.refs_3_), channel_id=1, source_target_pairs={{0,1},{1,2},{2,3},{3,4},{4,5},{5,6},{6,7},{7,0},{8,9},{9,10},{10,1... | collective-permute-start | bytes 1572872 | tf_op jit(solution)/shard_map/ppermute | solution.py:223
  47.4 30.9 %copy-start.12 = (f32[2,64,512]{2,1,0:T(8,128)}, f32[2,64,512]{2,1,0:T(8,128)S(1)}, u32[]{:S(2)}) copy-start(f32[2,64,512]{2,1,0:T(8,128)S(1)} %collective-permute-done.11.refs_13_) | copy-start | bytes 786436
  47.4 43.2 %collective-permute-start.20 = (f32[4,64,512]{2,1,0:T(8,128)}, f32[4,64,512]{2,1,0:T(8,128)S(1)}, u32[]{:S(2)}, u32[]{:S(2)}) collective-permute-start(f32[4,64,512]{2,1,0:T(8,128)} %collective-permute-done.5.refs_6_), channel_id=1, source_target_pairs={{0,7},{1,0},{2,1},{3,2},{4,3},{5,4},{6,5},{7,6},{8,15},{9,8},{10,9... | collective-permute-start | bytes 1572872 | tf_op jit(solution)/shard_map/ppermute | solution.py:223
  63.5 14.8 %copy-start.13 = (f32[2,64,512]{2,1,0:T(8,128)}, f32[2,64,512]{2,1,0:T(8,128)S(1)}, u32[]{:S(2)}) copy-start(f32[2,64,512]{2,1,0:T(8,128)S(1)} %collective-permute-done.10.refs_12_) | copy-start | bytes 786436
  63.5 7.9 %collective-permute-start.12 = (f32[1,64,512]{2,1,0:T(8,128)S(1)}, f32[1,64,512]{2,1,0:T(8,128)S(1)}, u32[]{:S(2)}, u32[]{:S(2)}) collective-permute-start(f32[1,64,512]{2,1,0:T(8,128)S(1)} %slice.33), channel_id=1, source_target_pairs={{0,7},{1,0},{2,1},{3,2},{4,3},{5,4},{6,5},{7,6},{8,15},{9,8},{10,9... | collective-permute-start | bytes 393224 | tf_op jit(solution)/shard_map/ppermute | solution.py:223
  71.4 6.9 %copy-start.18 = (f32[1,64,512]{2,1,0:T(8,128)}, f32[1,64,512]{2,1,0:T(8,128)S(1)}, u32[]{:S(2)}) copy-start(f32[1,64,512]{2,1,0:T(8,128)S(1)} %collective-permute-done.12.refs_14_) | copy-start | bytes 393220
  71.4 6.8 %collective-permute-start.13 = (f32[1,64,512]{2,1,0:T(8,128)}, f32[1,64,512]{2,1,0:T(8,128)S(1)}, u32[]{:S(2)}, u32[]{:S(2)}) collective-permute-start(f32[1,64,512]{2,1,0:T(8,128)} %slice.34), channel_id=1, source_target_pairs={{0,1},{1,2},{2,3},{3,4},{4,5},{5,6},{6,7},{7,0},{8,9},{9,10},{10,1... | collective-permute-start | bytes 393224 | tf_op jit(solution)/shard_map/ppermute | solution.py:223
  78.2 0.7 copy-start.19
  78.9 11.7 %copy-start.3 = (s32[64,10]{0,1:T(8,128)S(1)}, s32[64,10]{0,1:T(8,128)}, u32[]{:S(2)}) copy-start(s32[64,10]{0,1:T(8,128)} %param.8) | copy-start | bytes 7684
  78.9 11.7 %copy-start.4 = (s32[64,4]{0,1:T(4,128)S(1)}, s32[64,4]{0,1:T(4,128)}, u32[]{:S(2)}) copy-start(s32[64,4]{0,1:T(4,128)} %param.7) | copy-start | bytes 3076
  78.9 11.7 %copy-start.5 = (s32[2]{0:T(128)S(1)}, s32[2]{0:T(128)}, u32[]{:S(2)}) copy-start(s32[2]{0:T(128)} %pad_add_fusion.pos.meta) | copy-start | bytes 28
  90.6 1.6 %copy-start = (bf16[2,1024,512]{2,1,0:T(8,128)(2,1)S(1)}, bf16[2,1024,512]{2,1,0:T(8,128)(2,1)}, u32[]{:S(2)}) copy-start(bf16[2,1024,512]{2,1,0:T(8,128)(2,1)} %get-tuple-element.13.refs_4_) | copy-start | bytes 6291460
  92.1 1.6 %copy-start.1 = (bf16[2,2,256,1024]{3,2,1,0:T(8,128)(2,1)S(1)}, bf16[2,2,256,1024]{3,2,1,0:T(8,128)(2,1)}, u32[]{:S(2)}) copy-start(bf16[2,2,256,1024]{3,2,1,0:T(8,128)(2,1)} %get-tuple-element.14.refs_5_) | copy-start | bytes 6291460
  101.8 2.4 %collective-permute-start.21 = (f32[16,96,128]{2,1,0:T(8,128)S(1)}, f32[16,96,128]{2,1,0:T(8,128)S(1)}, u32[]{:S(2)}, u32[]{:S(2)}) collective-permute-start(f32[16,96,128]{2,1,0:T(8,128)S(1)} %get-tuple-element.16), channel_id=1, source_target_pairs={{0,8},{8,0},{16,24},{24,16},{32,40},{40,32},{48,56},{56,48},{64,72... | collective-permute-start | bytes 2359304 | tf_op jit(solution)/shard_map/ppermute | solution.py:226
  101.9 10.9 %collective-permute-start.14 = (f32[16,160,128]{2,1,0:T(8,128)}, f32[16,160,128]{2,1,0:T(8,128)}, u32[]{:S(2)}, u32[]{:S(2)}) collective-permute-start(f32[16,160,128]{2,1,0:T(8,128)} %get-tuple-element.12), channel_id=1, source_target_pairs={{0,8},{8,0},{16,24},{24,16},{32,40},{40,32},{48,56},{56,48},{64,72... | collective-permute-start | bytes 3932168 | tf_op jit(solution)/shard_map/ppermute | solution.py:226
  105.2 7.6 %copy-start.7 = (f32[16,160,128]{2,1,0:T(8,128)S(1)}, f32[16,160,128]{2,1,0:T(8,128)}, u32[]{:S(2)}) copy-start(f32[16,160,128]{2,1,0:T(8,128)} %get-tuple-element.11) | copy-start | bytes 3932164
  105.2 20.0 %all-to-all-start.1 = ((f32[16,96,128]{2,1,0:T(8,128)}), f32[16,96,128]{2,1,0:T(8,128)S(1)}, u32[]{:S(2)}, u32[]{:S(2)}) async-start(f32[16,96,128]{2,1,0:T(8,128)} %add.7), calls=%async_computation.1 | async-start | bytes 1572864 | tf_op jit(solution)/shard_map/all_to_all | solution.py:230
  125.2 23.3 %all-to-all-start = ((f32[16,160,128]{2,1,0:T(8,128)}), f32[16,160,128]{2,1,0:T(8,128)S(1)}, u32[]{:S(2)}, u32[]{:S(2)}) async-start(f32[16,160,128]{2,1,0:T(8,128)} %add.6), calls=%async_computation | async-start | bytes 2621440 | tf_op jit(solution)/shard_map/all_to_all | solution.py:230
  131.2 25.2 %copy-start.2 = (f32[1,64,512]{2,1,0:T(8,128)S(1)}, f32[1,64,512]{2,1,0:T(8,128)}, u32[]{:S(2)}) copy-start(f32[1,64,512]{2,1,0:T(8,128)} %anc.1) | copy-start | bytes 393220
  131.3 25.2 %collective-permute-start.22 = (f32[64,128]{1,0:T(8,128)S(1)}, f32[64,128]{1,0:T(8,128)S(1)}, u32[]{:S(2)}, u32[]{:S(2)}) collective-permute-start(f32[64,128]{1,0:T(8,128)S(1)} %slice.36), channel_id=1, source_target_pairs={{0,1},{1,2},{2,3},{3,4},{4,5},{5,6},{6,7},{7,0},{8,9},{9,10},{10,1... | collective-permute-start | bytes 98312 | tf_op jit(solution)/shard_map/ppermute | solution.py:223
  131.6 24.8 %collective-permute-start.23 = (f32[64,128]{1,0:T(8,128)S(1)}, f32[64,128]{1,0:T(8,128)S(1)}, u32[]{:S(2)}, u32[]{:S(2)}) collective-permute-start(f32[64,128]{1,0:T(8,128)S(1)} %slice.36), channel_id=1, source_target_pairs={{0,7},{1,0},{2,1},{3,2},{4,3},{5,4},{6,5},{7,6},{8,15},{9,8},{10,9... | collective-permute-start | bytes 98312 | tf_op jit(solution)/shard_map/ppermute | solution.py:223
  148.5 8.0 %collective-permute-start.15 = (f32[64,128]{1,0:T(8,128)S(1)}, f32[64,128]{1,0:T(8,128)S(1)}, u32[]{:S(2)}, u32[]{:S(2)}) collective-permute-start(f32[64,128]{1,0:T(8,128)S(1)} %slice.35), channel_id=1, source_target_pairs={{0,1},{1,2},{2,3},{3,4},{4,5},{5,6},{6,7},{7,0},{8,9},{9,10},{10,1... | collective-permute-start | bytes 98312 | tf_op jit(solution)/shard_map/ppermute | solution.py:223
  148.6 7.9 %collective-permute-start.16 = (f32[64,128]{1,0:T(8,128)S(1)}, f32[64,128]{1,0:T(8,128)S(1)}, u32[]{:S(2)}, u32[]{:S(2)}) collective-permute-start(f32[64,128]{1,0:T(8,128)S(1)} %slice.35), channel_id=1, source_target_pairs={{0,7},{1,0},{2,1},{3,2},{4,3},{5,4},{6,5},{7,6},{8,15},{9,8},{10,9... | collective-permute-start | bytes 98312 | tf_op jit(solution)/shard_map/ppermute | solution.py:223
  151.8 4.6 %collective-permute-start.24 = (f32[32,128]{1,0:T(8,128)S(1)}, f32[32,128]{1,0:T(8,128)S(1)}, u32[]{:S(2)}, u32[]{:S(2)}) collective-permute-start(f32[32,128]{1,0:T(8,128)S(1)} %slice.37), channel_id=1, source_target_pairs={{0,6},{1,7},{2,0},{3,1},{4,2},{5,3},{6,4},{7,5},{8,14},{9,15},{10,... | collective-permute-start | bytes 49160 | tf_op jit(solution)/shard_map/ppermute | solution.py:223

commit v2 on v1

--- a/solution.py
+++ b/solution.py
@@ -45,7 +45,8 @@
 
 def place(meta, s, p):
     tile = meta[10 + s * 10 + p]
-    return (tile + meta[1]) & 1, tile >> 1
+    first, second = tile >> 3, (tile >> 1) & 3
+    return (tile + meta[1]) & 1, jnp.where((tile & 1) == 0, ((first - second) & 3) * 4 + second, ((second - first) & 3) * 4 + first)
 
 
 def scale(x_ref, f3, s):
@@ -226,7 +227,10 @@
         return lax.ppermute(x, "wide", [(i, i ^ 1) for i in range(32)])
 
     def scatter(x):
-        groups = [[2 * i + c for i in range(16)] for c in range(2)]
+        groups = [
+            [((a + y) % 4 * 4 + y) * 2 for a in range(4) for y in range(4)],
+            [(x * 4 + (a + x) % 4) * 2 + 1 for a in range(4) for x in range(4)],
+        ]
         return lax.all_to_all(x, "wide", 0, 0, axis_index_groups=groups, tiled=True)
 
     chunks = [panels[BOUNDS[c] : BOUNDS[c + 1]] for c in range(CHUNKS)]

time: 159 us -> 159 us (level)
  no operation moved by 1% of the time
where the time goes in v2:
time: 159 us; the launch traced here: 158 us
  waiting for transfers between devices  81.9 us (52%)
  starting transfers between devices  43 us (27%)
  Pallas kernels  21 us (13%)
  other arithmetic  5.93 us (4%)
  local copies, waits for them, and re-layouts  5.65 us (4%)
    ppermute x23, waiting for transfers between devices, along(): return lax.ppermute(x, 'narrow', [(i, (i + d) % 8) for i in range(8)])  55.9 us
    ppermute x23, starting transfers between devices, along(): return lax.ppermute(x, 'narrow', [(i, (i + d) % 8) for i in range(8)])  29.6 us
    all_to_all x2, waiting for transfers between devices, scatter(): return lax.all_to_all(x, 'wide', 0, 0, axis_index_groups=groups, tiled=True)  24.3 us
    all_to_all x2, starting transfers between devices, scatter(): return lax.all_to_all(x, 'wide', 0, 0, axis_index_groups=groups, tiled=True)  12.8 us
    pallas_call x1, Pallas kernels, level(): near(*scalars, panels, *u1, *d1, factors, fu[1], fd[1], fu[2], fd[2], fu[...  11.6 us
    pallas_call x1, Pallas kernels, level(): keep2, send2 = far(*scalars, *u2, *d2, f3, n3)  8.05 us
    unnamed x40, local copies, waits for them, and re-layouts  3.87 us
  transfers between devices with their start and end apart: 27, of which 14 were waited for; matrix products, arithmetic and copies ran while one was open for 5% of the time, Pallas kernels for 7%

profile of v2, /device:TPU:2, one launch (start us, length us, event | category | flops | bytes accessed | tf_op | source)
XLA Modules:
  0.0 157.8 jit_solution(1467213615847384783)
XLA Ops:
  0.0 5.9 %collective-permute-start.7 = (f32[2,64,512]{2,1,0:T(8,128)}, f32[2,64,512]{2,1,0:T(8,128)S(1)}, u32[]{:S(2)}, u32[]{:S(2)}) collective-permute-start(f32[2,64,512]{2,1,0:T(8,128)} %refs_7_.1), channel_id=1, source_target_pairs={{0,7},{1,0},{2,1},{3,2},{4,3},{5,4},{6,5},{7,6},{8,15},{9,8},{10,9... | collective-permute-start | bytes 786440 | tf_op jit(solution)/shard_map/ppermute | solution.py:224
  5.9 0.0 collective-permute-start.6
  5.9 1.1 fusion
  6.9 0.1 collective-permute-start
  7.0 0.1 collective-permute-start.1
  7.1 3.3 %collective-permute-start.3 = (f32[2,64,512]{2,1,0:T(8,128)S(1)}, f32[2,64,512]{2,1,0:T(8,128)S(1)}, u32[]{:S(2)}, u32[]{:S(2)}) collective-permute-start(f32[2,64,512]{2,1,0:T(8,128)S(1)} %get-tuple-element.18), channel_id=1, source_target_pairs={{0,7},{1,0},{2,1},{3,2},{4,3},{5,4},{6,5},{7,6},{8,15},{9,8},{10,9... | collective-permute-start | bytes 786440 | tf_op jit(solution)/shard_map/ppermute | solution.py:224
  10.5 2.4 %collective-permute-done.7.refs_9_ = f32[2,64,512]{2,1,0:T(8,128)S(1)} collective-permute-done((f32[2,64,512]{2,1,0:T(8,128)}, f32[2,64,512]{2,1,0:T(8,128)S(1)}, u32[]{:S(2)}, u32[]{:S(2)}) %collective-permute-start.7) | collective-permute-done | bytes 262176 | tf_op jit(solution)/shard_map/ppermute | solution.py:224
  12.9 0.0 collective-permute-start.2
  12.9 3.6 %collective-permute-done.6.refs_8_ = f32[2,64,512]{2,1,0:T(8,128)S(1)} collective-permute-done((f32[2,64,512]{2,1,0:T(8,128)}, f32[2,64,512]{2,1,0:T(8,128)S(1)}, u32[]{:S(2)}, u32[]{:S(2)}) %collective-permute-start.6) | collective-permute-done | bytes 262176 | tf_op jit(solution)/shard_map/ppermute | solution.py:224
  16.5 0.1 collective-permute-start.5
  16.6 5.5 %collective-permute-done.refs_1_ = f32[2,64,512]{2,1,0:T(8,128)S(1)} collective-permute-done((f32[2,64,512]{2,1,0:T(8,128)S(1)}, f32[2,64,512]{2,1,0:T(8,128)S(1)}, u32[]{:S(2)}, u32[]{:S(2)}) %collective-permute-start) | collective-permute-done | bytes 262176 | tf_op jit(solution)/shard_map/ppermute | solution.py:224
  22.1 0.0 collective-permute-start.9
  22.1 5.6 %collective-permute-done.1.refs_2_ = f32[2,64,512]{2,1,0:T(8,128)S(1)} collective-permute-done((f32[2,64,512]{2,1,0:T(8,128)S(1)}, f32[2,64,512]{2,1,0:T(8,128)S(1)}, u32[]{:S(2)}, u32[]{:S(2)}) %collective-permute-start.1) | collective-permute-done | bytes 262176 | tf_op jit(solution)/shard_map/ppermute | solution.py:224
  27.7 0.0 collective-permute-start.4
  27.7 0.0 collective-permute-done.3.refs_4_
  27.7 2.0 %collective-permute-start.8 = (f32[2,64,512]{2,1,0:T(8,128)S(1)}, f32[2,64,512]{2,1,0:T(8,128)S(1)}, u32[]{:S(2)}, u32[]{:S(2)}) collective-permute-start(f32[2,64,512]{2,1,0:T(8,128)S(1)} %collective-permute-done.6.refs_8_), channel_id=1, source_target_pairs={{0,1},{1,2},{2,3},{3,4},{4,5},{5,6},{6,7},{7,0},{8,9},{9,10},{10,1... | collective-permute-start | bytes 786440 | tf_op jit(solution)/shard_map/ppermute | solution.py:224
  29.7 6.6 %collective-permute-done.9.refs_11_ = f32[2,64,512]{2,1,0:T(8,128)S(1)} collective-permute-done((f32[2,64,512]{2,1,0:T(8,128)S(1)}, f32[2,64,512]{2,1,0:T(8,128)S(1)}, u32[]{:S(2)}, u32[]{:S(2)}) %collective-permute-start.9) | collective-permute-done | bytes 262176 | tf_op jit(solution)/shard_map/ppermute | solution.py:224
  36.3 2.6 %collective-permute-start.11 = (f32[2,64,512]{2,1,0:T(8,128)S(1)}, f32[2,64,512]{2,1,0:T(8,128)S(1)}, u32[]{:S(2)}, u32[]{:S(2)}) collective-permute-start(f32[2,64,512]{2,1,0:T(8,128)S(1)} %collective-permute-done.9.refs_11_), channel_id=1, source_target_pairs={{0,7},{1,0},{2,1},{3,2},{4,3},{5,4},{6,5},{7,6},{8,15},{9,8},{10,9... | collective-permute-start | bytes 786440 | tf_op jit(solution)/shard_map/ppermute | solution.py:224
  38.9 0.9 pad_maximum_fusion
  39.8 1.8 %collective-permute-done.4.refs_5_ = f32[2,64,512]{2,1,0:T(8,128)S(1)} collective-permute-done((f32[2,64,512]{2,1,0:T(8,128)S(1)}, f32[2,64,512]{2,1,0:T(8,128)S(1)}, u32[]{:S(2)}, u32[]{:S(2)}) %collective-permute-start.4) | collective-permute-done | bytes 262176 | tf_op jit(solution)/shard_map/ppermute | solution.py:224
  41.6 0.0 collective-permute-start.17
  41.6 1.5 collective-permute-done.8.refs_10_
  43.1 0.4 collective-permute-start.10
  43.6 0.9 pad_maximum_fusion.1
  44.5 0.0 collective-permute-done.2.refs_3_
  44.5 2.9 %collective-permute-start.19 = (f32[4,64,512]{2,1,0:T(8,128)}, f32[4,64,512]{2,1,0:T(8,128)S(1)}, u32[]{:S(2)}, u32[]{:S(2)}) collective-permute-start(f32[4,64,512]{2,1,0:T(8,128)} %pad_maximum_fusion.1), channel_id=1, source_target_pairs={{0,7},{1,0},{2,1},{3,2},{4,3},{5,4},{6,5},{7,6},{8,15},{9,8},{10,9... | collective-permute-start | bytes 1572872 | tf_op jit(solution)/shard_map/ppermute | solution.py:224
  47.3 0.0 collective-permute-done.5.refs_6_
  47.3 0.0 collective-permute-start.18
  47.3 0.0 collective-permute-done.11.refs_13_
  47.4 3.5 %collective-permute-start.20 = (f32[4,64,512]{2,1,0:T(8,128)}, f32[4,64,512]{2,1,0:T(8,128)S(1)}, u32[]{:S(2)}, u32[]{:S(2)}) collective-permute-start(f32[4,64,512]{2,1,0:T(8,128)} %collective-permute-done.5.refs_6_), channel_id=1, source_target_pairs={{0,7},{1,0},{2,1},{3,2},{4,3},{5,4},{6,5},{7,6},{8,15},{9,8},{10,9... | collective-permute-start | bytes 1572872 | tf_op jit(solution)/shard_map/ppermute | solution.py:224
  50.9 12.6 %collective-permute-done.10.refs_12_ = f32[2,64,512]{2,1,0:T(8,128)S(1)} collective-permute-done((f32[2,64,512]{2,1,0:T(8,128)S(1)}, f32[2,64,512]{2,1,0:T(8,128)S(1)}, u32[]{:S(2)}, u32[]{:S(2)}) %collective-permute-start.10) | collective-permute-done | bytes 262176 | tf_op jit(solution)/shard_map/ppermute | solution.py:224
  63.5 1.7 %collective-permute-start.12 = (f32[1,64,512]{2,1,0:T(8,128)S(1)}, f32[1,64,512]{2,1,0:T(8,128)S(1)}, u32[]{:S(2)}, u32[]{:S(2)}) collective-permute-start(f32[1,64,512]{2,1,0:T(8,128)S(1)} %slice.33), channel_id=1, source_target_pairs={{0,7},{1,0},{2,1},{3,2},{4,3},{5,4},{6,5},{7,6},{8,15},{9,8},{10,9... | collective-permute-start | bytes 393224 | tf_op jit(solution)/shard_map/ppermute | solution.py:224
  65.2 0.7 slice.34
  65.8 5.5 %collective-permute-done.12.refs_14_ = f32[1,64,512]{2,1,0:T(8,128)S(1)} collective-permute-done((f32[1,64,512]{2,1,0:T(8,128)S(1)}, f32[1,64,512]{2,1,0:T(8,128)S(1)}, u32[]{:S(2)}, u32[]{:S(2)}) %collective-permute-start.12) | collective-permute-done | bytes 131104 | tf_op jit(solution)/shard_map/ppermute | solution.py:224
  71.4 0.0 collective-permute-start.13
  71.4 0.6 pad_add_fusion.pos.meta
  71.9 6.3 %collective-permute-done.13.refs_15_ = f32[1,64,512]{2,1,0:T(8,128)S(1)} collective-permute-done((f32[1,64,512]{2,1,0:T(8,128)}, f32[1,64,512]{2,1,0:T(8,128)S(1)}, u32[]{:S(2)}, u32[]{:S(2)}) %collective-permute-start.13) | collective-permute-done | bytes 131104 | tf_op jit(solution)/shard_map/ppermute | solution.py:224
  78.2 0.6 copy-done.19
  78.9 11.6 %near.1 = (f32[16,160,128]{2,1,0:T(8,128)}, f32[16,160,128]{2,1,0:T(8,128)}, bf16[2,1024,512]{2,1,0:T(8,128)(2,1)}, bf16[2,2,256,1024]{3,2,1,0:T(8,128)(2,1)}) custom-call(s32[2]{0:T(128)} %pad_add_fusion.pos.meta, s32[4,64]{1,0:T(4,128)} %bitcast.6, s32[10,64]{1,0:T(8,128)} %bitcast.4, f32[8,64,512]{2,1,0:T(8,128)} %refs_0_.1, f32[2,64,512]{2,1,0:T(8,128)} %copy-done.8, ...), custom_call_target="tpu_custom_call" | custom-call | tf_op jit(solution)/shard_map/near/pallas_call | solution.py:278
  90.5 0.0 collective-permute-done.17.refs_0_
  90.5 0.0 collective-permute-done.19.refs_2_
  90.5 0.0 collective-permute-done.18.refs_1_
  90.5 0.0 collective-permute-done.20.refs_3_
  90.6 1.6 %copy-done = bf16[2,1024,512]{2,1,0:T(8,128)(2,1)S(1)} copy-done((bf16[2,1024,512]{2,1,0:T(8,128)(2,1)S(1)}, bf16[2,1024,512]{2,1,0:T(8,128)(2,1)}, u32[]{:S(2)}) %copy-start) | copy-done | bytes 2097176
  92.2 1.6 %copy-done.1 = bf16[2,2,256,1024]{3,2,1,0:T(8,128)(2,1)S(1)} copy-done((bf16[2,2,256,1024]{3,2,1,0:T(8,128)(2,1)S(1)}, bf16[2,2,256,1024]{3,2,1,0:T(8,128)(2,1)}, u32[]{:S(2)}) %copy-start.1) | copy-done | bytes 2097176
  93.8 8.1 %far.1 = (f32[16,96,128]{2,1,0:T(8,128)S(1)}, f32[16,96,128]{2,1,0:T(8,128)S(1)}) custom-call(s32[2]{0:T(128)S(1)} %copy-done.5, s32[4,64]{1,0:T(4,128)S(1)} %bitcast.7, s32[10,64]{1,0:T(8,128)S(1)} %bitcast.5, f32[4,64,512]{2,1,0:T(8,128)S(1)} %collective-permute-done.17.refs_0_, f32[4,64,512]{2,1,0:T(8,128)S(1)} %collective-permute-done.18.refs_1_, ...), custom_call_target="tpu_custom_call" | custom-call | tf_op jit(solution)/shard_map/far/pallas_call | solution.py:303
  101.8 0.1 collective-permute-start.21
  101.9 0.5 collective-permute-start.14
  102.4 1.8 %collective-permute-done.21 = f32[16,96,128]{2,1,0:T(8,128)S(1)} collective-permute-done((f32[16,96,128]{2,1,0:T(8,128)S(1)}, f32[16,96,128]{2,1,0:T(8,128)S(1)}, u32[]{:S(2)}, u32[]{:S(2)}) %collective-permute-start.21) | collective-permute-done | bytes 786464 | tf_op jit(solution)/shard_map/ppermute | solution.py:227
  104.2 1.0 add.7
  105.2 7.6 %all-to-all-start.1 = ((f32[16,96,128]{2,1,0:T(8,128)}), f32[16,96,128]{2,1,0:T(8,128)S(1)}, u32[]{:S(2)}, u32[]{:S(2)}) async-start(f32[16,96,128]{2,1,0:T(8,128)} %add.7), calls=%async_computation.1 | async-start | bytes 1572864 | tf_op jit(solution)/shard_map/all_to_all | solution.py:234
  112.8 2.5 %add.6 = f32[16,160,128]{2,1,0:T(8,128)} add(f32[16,160,128]{2,1,0:T(8,128)S(1)} %copy-done.7, f32[16,160,128]{2,1,0:T(8,128)} %collective-permute-done.14) | non-fusion elementwise | flops 327680 | bytes 3932160 | tf_op jit(solution)/shard_map/add | solution.py:279
  115.3 10.4 %all-to-all-done.1 = f32[16,96,128]{2,1,0:T(8,128)S(1)} async-done(((f32[16,96,128]{2,1,0:T(8,128)}), f32[16,96,128]{2,1,0:T(8,128)S(1)}, u32[]{:S(2)}, u32[]{:S(2)}) %all-to-all-start.1) | async-done | bytes 786464 | tf_op jit(solution)/shard_map/all_to_all | solution.py:234
  125.7 5.2 %all-to-all-start = ((f32[16,160,128]{2,1,0:T(8,128)}), f32[16,160,128]{2,1,0:T(8,128)S(1)}, u32[]{:S(2)}, u32[]{:S(2)}) async-start(f32[16,160,128]{2,1,0:T(8,128)} %add.6), calls=%async_computation | async-start | bytes 2621440 | tf_op jit(solution)/shard_map/all_to_all | solution.py:234
  131.0 0.3 collective-permute-start.22
  131.3 3.2 %collective-permute-start.23 = (f32[64,128]{1,0:T(8,128)S(1)}, f32[64,128]{1,0:T(8,128)S(1)}, u32[]{:S(2)}, u32[]{:S(2)}) collective-permute-start(f32[64,128]{1,0:T(8,128)S(1)} %slice.36), channel_id=1, source_target_pairs={{0,7},{1,0},{2,1},{3,2},{4,3},{5,4},{6,5},{7,6},{8,15},{9,8},{10,9... | collective-permute-start | bytes 98312 | tf_op jit(solution)/shard_map/ppermute | solution.py:224
  134.5 13.9 %all-to-all-done = f32[16,160,128]{2,1,0:T(8,128)S(1)} async-done(((f32[16,160,128]{2,1,0:T(8,128)}), f32[16,160,128]{2,1,0:T(8,128)S(1)}, u32[]{:S(2)}, u32[]{:S(2)}) %all-to-all-start) | async-done | bytes 1310752 | tf_op jit(solution)/shard_map/all_to_all | solution.py:234
  148.4 0.1 reduce_sum.18.near
  148.5 0.1 collective-permute-start.15
  148.6 3.2 %collective-permute-start.16 = (f32[64,128]{1,0:T(8,128)S(1)}, f32[64,128]{1,0:T(8,128)S(1)}, u32[]{:S(2)}, u32[]{:S(2)}) collective-permute-start(f32[64,128]{1,0:T(8,128)S(1)} %slice.35), channel_id=1, source_target_pairs={{0,7},{1,0},{2,1},{3,2},{4,3},{5,4},{6,5},{7,6},{8,15},{9,8},{10,9... | collective-permute-start | bytes 98312 | tf_op jit(solution)/shard_map/ppermute | solution.py:224
  151.8 0.2 collective-permute-start.24
  152.0 4.4 %collective-permute-done.24.cd = f32[32,128]{1,0:T(8,128)S(1)} collective-permute-done((f32[32,128]{1,0:T(8,128)S(1)}, f32[32,128]{1,0:T(8,128)S(1)}, u32[]{:S(2)}, u32[]{:S(2)}) %collective-permute-start.24) | collective-permute-done | bytes 16416 | tf_op jit(solution)/shard_map/ppermute | solution.py:224
  156.4 0.0 collective-permute-done.16.ed
  156.5 1.3 final.1
  (47 shorter events, 0.2 us)
Async XLA Ops:
  0.0 10.4 %copy-start.6 = (f32[8,64,512]{2,1,0:T(8,128)S(1)}, f32[8,64,512]{2,1,0:T(8,128)}, u32[]{:S(2)}) copy-start(f32[8,64,512]{2,1,0:T(8,128)} %refs_0_.1) | copy-start | bytes 3145732
  0.0 12.9 %collective-permute-start.7 = (f32[2,64,512]{2,1,0:T(8,128)}, f32[2,64,512]{2,1,0:T(8,128)S(1)}, u32[]{:S(2)}, u32[]{:S(2)}) collective-permute-start(f32[2,64,512]{2,1,0:T(8,128)} %refs_7_.1), channel_id=1, source_target_pairs={{0,7},{1,0},{2,1},{3,2},{4,3},{5,4},{6,5},{7,6},{8,15},{9,8},{10,9... | collective-permute-start | bytes 786440 | tf_op jit(solution)/shard_map/ppermute | solution.py:224
  5.9 10.6 %collective-permute-start.6 = (f32[2,64,512]{2,1,0:T(8,128)}, f32[2,64,512]{2,1,0:T(8,128)S(1)}, u32[]{:S(2)}, u32[]{:S(2)}) collective-permute-start(f32[2,64,512]{2,1,0:T(8,128)} %refs_7_.1), channel_id=1, source_target_pairs={{0,1},{1,2},{2,3},{3,4},{4,5},{5,6},{6,7},{7,0},{8,9},{9,10},{10,1... | collective-permute-start | bytes 786440 | tf_op jit(solution)/shard_map/ppermute | solution.py:224
  6.9 15.1 %collective-permute-start = (f32[2,64,512]{2,1,0:T(8,128)S(1)}, f32[2,64,512]{2,1,0:T(8,128)S(1)}, u32[]{:S(2)}, u32[]{:S(2)}) collective-permute-start(f32[2,64,512]{2,1,0:T(8,128)S(1)} %get-tuple-element.18), channel_id=1, source_target_pairs={{0,1},{1,2},{2,3},{3,4},{4,5},{5,6},{6,7},{7,0},{8,9},{9,10},{10,1... | collective-permute-start | bytes 786440 | tf_op jit(solution)/shard_map/ppermute | solution.py:224
  7.0 20.7 %collective-permute-start.1 = (f32[2,64,512]{2,1,0:T(8,128)S(1)}, f32[2,64,512]{2,1,0:T(8,128)S(1)}, u32[]{:S(2)}, u32[]{:S(2)}) collective-permute-start(f32[2,64,512]{2,1,0:T(8,128)S(1)} %get-tuple-element.17), channel_id=1, source_target_pairs={{0,1},{1,2},{2,3},{3,4},{4,5},{5,6},{6,7},{7,0},{8,9},{9,10},{10,1... | collective-permute-start | bytes 786440 | tf_op jit(solution)/shard_map/ppermute | solution.py:224
  7.1 20.6 %collective-permute-start.3 = (f32[2,64,512]{2,1,0:T(8,128)S(1)}, f32[2,64,512]{2,1,0:T(8,128)S(1)}, u32[]{:S(2)}, u32[]{:S(2)}) collective-permute-start(f32[2,64,512]{2,1,0:T(8,128)S(1)} %get-tuple-element.18), channel_id=1, source_target_pairs={{0,7},{1,0},{2,1},{3,2},{4,3},{5,4},{6,5},{7,6},{8,15},{9,8},{10,9... | collective-permute-start | bytes 786440 | tf_op jit(solution)/shard_map/ppermute | solution.py:224
  12.9 31.6 %copy-start.14 = (f32[2,64,512]{2,1,0:T(8,128)}, f32[2,64,512]{2,1,0:T(8,128)S(1)}, u32[]{:S(2)}) copy-start(f32[2,64,512]{2,1,0:T(8,128)S(1)} %collective-permute-done.7.refs_9_) | copy-start | bytes 786436
  12.9 31.6 %collective-permute-start.2 = (f32[4,64,512]{2,1,0:T(8,128)S(1)}, f32[4,64,512]{2,1,0:T(8,128)}, u32[]{:S(2)}, u32[]{:S(2)}) collective-permute-start(f32[4,64,512]{2,1,0:T(8,128)S(1)} %slice.27), channel_id=1, source_target_pairs={{0,1},{1,2},{2,3},{3,4},{4,5},{5,6},{6,7},{7,0},{8,9},{9,10},{10,1... | collective-permute-start | bytes 1572872 | tf_op jit(solution)/shard_map/ppermute | solution.py:224
  16.5 30.9 %copy-start.15 = (f32[2,64,512]{2,1,0:T(8,128)}, f32[2,64,512]{2,1,0:T(8,128)S(1)}, u32[]{:S(2)}) copy-start(f32[2,64,512]{2,1,0:T(8,128)S(1)} %collective-permute-done.6.refs_8_) | copy-start | bytes 786436
  16.5 30.9 %collective-permute-start.5 = (f32[4,64,512]{2,1,0:T(8,128)S(1)}, f32[4,64,512]{2,1,0:T(8,128)}, u32[]{:S(2)}, u32[]{:S(2)}) collective-permute-start(f32[4,64,512]{2,1,0:T(8,128)S(1)} %slice.27), channel_id=1, source_target_pairs={{0,7},{1,0},{2,1},{3,2},{4,3},{5,4},{6,5},{7,6},{8,15},{9,8},{10,9... | collective-permute-start | bytes 1572872 | tf_op jit(solution)/shard_map/ppermute | solution.py:224
  22.1 43.8 %copy-start.8 = (f32[2,64,512]{2,1,0:T(8,128)}, f32[2,64,512]{2,1,0:T(8,128)S(1)}, u32[]{:S(2)}) copy-start(f32[2,64,512]{2,1,0:T(8,128)S(1)} %collective-permute-done.refs_1_) | copy-start | bytes 786436
  22.1 14.2 %collective-permute-start.9 = (f32[2,64,512]{2,1,0:T(8,128)S(1)}, f32[2,64,512]{2,1,0:T(8,128)S(1)}, u32[]{:S(2)}, u32[]{:S(2)}) collective-permute-start(f32[2,64,512]{2,1,0:T(8,128)S(1)} %collective-permute-done.7.refs_9_), channel_id=1, source_target_pairs={{0,7},{1,0},{2,1},{3,2},{4,3},{5,4},{6,5},{7,6},{8,15},{9,8},{10,9... | collective-permute-start | bytes 786440 | tf_op jit(solution)/shard_map/ppermute | solution.py:224
  27.7 38.1 %copy-start.9 = (f32[2,64,512]{2,1,0:T(8,128)}, f32[2,64,512]{2,1,0:T(8,128)S(1)}, u32[]{:S(2)}) copy-start(f32[2,64,512]{2,1,0:T(8,128)S(1)} %collective-permute-done.1.refs_2_) | copy-start | bytes 786436
  27.7 13.9 %collective-permute-start.4 = (f32[2,64,512]{2,1,0:T(8,128)S(1)}, f32[2,64,512]{2,1,0:T(8,128)S(1)}, u32[]{:S(2)}, u32[]{:S(2)}) collective-permute-start(f32[2,64,512]{2,1,0:T(8,128)S(1)} %get-tuple-element.17), channel_id=1, source_target_pairs={{0,7},{1,0},{2,1},{3,2},{4,3},{5,4},{6,5},{7,6},{8,15},{9,8},{10,9... | collective-permute-start | bytes 786440 | tf_op jit(solution)/shard_map/ppermute | solution.py:224
  27.7 16.7 %copy-start.10 = (f32[2,64,512]{2,1,0:T(8,128)}, f32[2,64,512]{2,1,0:T(8,128)S(1)}, u32[]{:S(2)}) copy-start(f32[2,64,512]{2,1,0:T(8,128)S(1)} %collective-permute-done.3.refs_4_) | copy-start | bytes 786436
  27.7 15.4 %collective-permute-start.8 = (f32[2,64,512]{2,1,0:T(8,128)S(1)}, f32[2,64,512]{2,1,0:T(8,128)S(1)}, u32[]{:S(2)}, u32[]{:S(2)}) collective-permute-start(f32[2,64,512]{2,1,0:T(8,128)S(1)} %collective-permute-done.6.refs_8_), channel_id=1, source_target_pairs={{0,1},{1,2},{2,3},{3,4},{4,5},{5,6},{6,7},{7,0},{8,9},{9,10},{10,1... | collective-permute-start | bytes 786440 | tf_op jit(solution)/shard_map/ppermute | solution.py:224
  36.3 29.5 %copy-start.16 = (f32[2,64,512]{2,1,0:T(8,128)}, f32[2,64,512]{2,1,0:T(8,128)S(1)}, u32[]{:S(2)}) copy-start(f32[2,64,512]{2,1,0:T(8,128)S(1)} %collective-permute-done.9.refs_11_) | copy-start | bytes 786436
  36.3 11.0 %collective-permute-start.11 = (f32[2,64,512]{2,1,0:T(8,128)S(1)}, f32[2,64,512]{2,1,0:T(8,128)S(1)}, u32[]{:S(2)}, u32[]{:S(2)}) collective-permute-start(f32[2,64,512]{2,1,0:T(8,128)S(1)} %collective-permute-done.9.refs_11_), channel_id=1, source_target_pairs={{0,7},{1,0},{2,1},{3,2},{4,3},{5,4},{6,5},{7,6},{8,15},{9,8},{10,9... | collective-permute-start | bytes 786440 | tf_op jit(solution)/shard_map/ppermute | solution.py:224
  41.6 36.6 %copy-start.11 = (f32[2,64,512]{2,1,0:T(8,128)}, f32[2,64,512]{2,1,0:T(8,128)S(1)}, u32[]{:S(2)}) copy-start(f32[2,64,512]{2,1,0:T(8,128)S(1)} %collective-permute-done.4.refs_5_) | copy-start | bytes 786436
  41.6 48.9 %collective-permute-start.17 = (f32[4,64,512]{2,1,0:T(8,128)}, f32[4,64,512]{2,1,0:T(8,128)S(1)}, u32[]{:S(2)}, u32[]{:S(2)}) collective-permute-start(f32[4,64,512]{2,1,0:T(8,128)} %pad_maximum_fusion), channel_id=1, source_target_pairs={{0,1},{1,2},{2,3},{3,4},{4,5},{5,6},{6,7},{7,0},{8,9},{9,10},{10,1... | collective-permute-start | bytes 1572872 | tf_op jit(solution)/shard_map/ppermute | solution.py:224
  43.1 28.2 %copy-start.17 = (f32[2,64,512]{2,1,0:T(8,128)}, f32[2,64,512]{2,1,0:T(8,128)S(1)}, u32[]{:S(2)}) copy-start(f32[2,64,512]{2,1,0:T(8,128)S(1)} %collective-permute-done.8.refs_10_) | copy-start | bytes 786436
  43.1 20.3 %collective-permute-start.10 = (f32[2,64,512]{2,1,0:T(8,128)S(1)}, f32[2,64,512]{2,1,0:T(8,128)S(1)}, u32[]{:S(2)}, u32[]{:S(2)}) collective-permute-start(f32[2,64,512]{2,1,0:T(8,128)S(1)} %collective-permute-done.8.refs_10_), channel_id=1, source_target_pairs={{0,1},{1,2},{2,3},{3,4},{4,5},{5,6},{6,7},{7,0},{8,9},{9,10},{10,1... | collective-permute-start | bytes 786440 | tf_op jit(solution)/shard_map/ppermute | solution.py:224
  44.5 46.1 %collective-permute-start.19 = (f32[4,64,512]{2,1,0:T(8,128)}, f32[4,64,512]{2,1,0:T(8,128)S(1)}, u32[]{:S(2)}, u32[]{:S(2)}) collective-permute-start(f32[4,64,512]{2,1,0:T(8,128)} %pad_maximum_fusion.1), channel_id=1, source_target_pairs={{0,7},{1,0},{2,1},{3,2},{4,3},{5,4},{6,5},{7,6},{8,15},{9,8},{10,9... | collective-permute-start | bytes 1572872 | tf_op jit(solution)/shard_map/ppermute | solution.py:224
  47.3 43.2 %collective-permute-start.18 = (f32[4,64,512]{2,1,0:T(8,128)}, f32[4,64,512]{2,1,0:T(8,128)S(1)}, u32[]{:S(2)}, u32[]{:S(2)}) collective-permute-start(f32[4,64,512]{2,1,0:T(8,128)} %collective-permute-done.2.refs_3_), channel_id=1, source_target_pairs={{0,1},{1,2},{2,3},{3,4},{4,5},{5,6},{6,7},{7,0},{8,9},{9,10},{10,1... | collective-permute-start | bytes 1572872 | tf_op jit(solution)/shard_map/ppermute | solution.py:224
  47.4 30.9 %copy-start.12 = (f32[2,64,512]{2,1,0:T(8,128)}, f32[2,64,512]{2,1,0:T(8,128)S(1)}, u32[]{:S(2)}) copy-start(f32[2,64,512]{2,1,0:T(8,128)S(1)} %collective-permute-done.11.refs_13_) | copy-start | bytes 786436
  47.4 43.2 %collective-permute-start.20 = (f32[4,64,512]{2,1,0:T(8,128)}, f32[4,64,512]{2,1,0:T(8,128)S(1)}, u32[]{:S(2)}, u32[]{:S(2)}) collective-permute-start(f32[4,64,512]{2,1,0:T(8,128)} %collective-permute-done.5.refs_6_), channel_id=1, source_target_pairs={{0,7},{1,0},{2,1},{3,2},{4,3},{5,4},{6,5},{7,6},{8,15},{9,8},{10,9... | collective-permute-start | bytes 1572872 | tf_op jit(solution)/shard_map/ppermute | solution.py:224
  63.5 14.8 %copy-start.13 = (f32[2,64,512]{2,1,0:T(8,128)}, f32[2,64,512]{2,1,0:T(8,128)S(1)}, u32[]{:S(2)}) copy-start(f32[2,64,512]{2,1,0:T(8,128)S(1)} %collective-permute-done.10.refs_12_) | copy-start | bytes 786436
  63.5 7.9 %collective-permute-start.12 = (f32[1,64,512]{2,1,0:T(8,128)S(1)}, f32[1,64,512]{2,1,0:T(8,128)S(1)}, u32[]{:S(2)}, u32[]{:S(2)}) collective-permute-start(f32[1,64,512]{2,1,0:T(8,128)S(1)} %slice.33), channel_id=1, source_target_pairs={{0,7},{1,0},{2,1},{3,2},{4,3},{5,4},{6,5},{7,6},{8,15},{9,8},{10,9... | collective-permute-start | bytes 393224 | tf_op jit(solution)/shard_map/ppermute | solution.py:224
  71.4 6.9 %copy-start.18 = (f32[1,64,512]{2,1,0:T(8,128)}, f32[1,64,512]{2,1,0:T(8,128)S(1)}, u32[]{:S(2)}) copy-start(f32[1,64,512]{2,1,0:T(8,128)S(1)} %collective-permute-done.12.refs_14_) | copy-start | bytes 393220
  71.4 6.8 %collective-permute-start.13 = (f32[1,64,512]{2,1,0:T(8,128)}, f32[1,64,512]{2,1,0:T(8,128)S(1)}, u32[]{:S(2)}, u32[]{:S(2)}) collective-permute-start(f32[1,64,512]{2,1,0:T(8,128)} %slice.34), channel_id=1, source_target_pairs={{0,1},{1,2},{2,3},{3,4},{4,5},{5,6},{6,7},{7,0},{8,9},{9,10},{10,1... | collective-permute-start | bytes 393224 | tf_op jit(solution)/shard_map/ppermute | solution.py:224
  78.2 0.7 copy-start.19
  78.9 11.7 %copy-start.3 = (s32[64,10]{0,1:T(8,128)S(1)}, s32[64,10]{0,1:T(8,128)}, u32[]{:S(2)}) copy-start(s32[64,10]{0,1:T(8,128)} %param.8) | copy-start | bytes 7684
  78.9 11.7 %copy-start.4 = (s32[64,4]{0,1:T(4,128)S(1)}, s32[64,4]{0,1:T(4,128)}, u32[]{:S(2)}) copy-start(s32[64,4]{0,1:T(4,128)} %param.7) | copy-start | bytes 3076
  78.9 11.7 %copy-start.5 = (s32[2]{0:T(128)S(1)}, s32[2]{0:T(128)}, u32[]{:S(2)}) copy-start(s32[2]{0:T(128)} %pad_add_fusion.pos.meta) | copy-start | bytes 28
  90.6 1.6 %copy-start = (bf16[2,1024,512]{2,1,0:T(8,128)(2,1)S(1)}, bf16[2,1024,512]{2,1,0:T(8,128)(2,1)}, u32[]{:S(2)}) copy-start(bf16[2,1024,512]{2,1,0:T(8,128)(2,1)} %get-tuple-element.13.refs_4_) | copy-start | bytes 6291460
  92.2 1.6 %copy-start.1 = (bf16[2,2,256,1024]{3,2,1,0:T(8,128)(2,1)S(1)}, bf16[2,2,256,1024]{3,2,1,0:T(8,128)(2,1)}, u32[]{:S(2)}) copy-start(bf16[2,2,256,1024]{3,2,1,0:T(8,128)(2,1)} %get-tuple-element.14.refs_5_) | copy-start | bytes 6291460
  101.8 2.4 %collective-permute-start.21 = (f32[16,96,128]{2,1,0:T(8,128)S(1)}, f32[16,96,128]{2,1,0:T(8,128)S(1)}, u32[]{:S(2)}, u32[]{:S(2)}) collective-permute-start(f32[16,96,128]{2,1,0:T(8,128)S(1)} %get-tuple-element.16), channel_id=1, source_target_pairs={{0,8},{8,0},{16,24},{24,16},{32,40},{40,32},{48,56},{56,48},{64,72... | collective-permute-start | bytes 2359304 | tf_op jit(solution)/shard_map/ppermute | solution.py:227
  101.9 10.9 %collective-permute-start.14 = (f32[16,160,128]{2,1,0:T(8,128)}, f32[16,160,128]{2,1,0:T(8,128)}, u32[]{:S(2)}, u32[]{:S(2)}) collective-permute-start(f32[16,160,128]{2,1,0:T(8,128)} %get-tuple-element.12), channel_id=1, source_target_pairs={{0,8},{8,0},{16,24},{24,16},{32,40},{40,32},{48,56},{56,48},{64,72... | collective-permute-start | bytes 3932168 | tf_op jit(solution)/shard_map/ppermute | solution.py:227
  105.2 7.6 %copy-start.7 = (f32[16,160,128]{2,1,0:T(8,128)S(1)}, f32[16,160,128]{2,1,0:T(8,128)}, u32[]{:S(2)}) copy-start(f32[16,160,128]{2,1,0:T(8,128)} %get-tuple-element.11) | copy-start | bytes 3932164
  105.2 20.5 %all-to-all-start.1 = ((f32[16,96,128]{2,1,0:T(8,128)}), f32[16,96,128]{2,1,0:T(8,128)S(1)}, u32[]{:S(2)}, u32[]{:S(2)}) async-start(f32[16,96,128]{2,1,0:T(8,128)} %add.7), calls=%async_computation.1 | async-start | bytes 1572864 | tf_op jit(solution)/shard_map/all_to_all | solution.py:234
  125.7 22.7 %all-to-all-start = ((f32[16,160,128]{2,1,0:T(8,128)}), f32[16,160,128]{2,1,0:T(8,128)S(1)}, u32[]{:S(2)}, u32[]{:S(2)}) async-start(f32[16,160,128]{2,1,0:T(8,128)} %add.6), calls=%async_computation | async-start | bytes 2621440 | tf_op jit(solution)/shard_map/all_to_all | solution.py:234
  130.9 25.6 %copy-start.2 = (f32[1,64,512]{2,1,0:T(8,128)S(1)}, f32[1,64,512]{2,1,0:T(8,128)}, u32[]{:S(2)}) copy-start(f32[1,64,512]{2,1,0:T(8,128)} %anc.1) | copy-start | bytes 393220
  131.0 25.5 %collective-permute-start.22 = (f32[64,128]{1,0:T(8,128)S(1)}, f32[64,128]{1,0:T(8,128)S(1)}, u32[]{:S(2)}, u32[]{:S(2)}) collective-permute-start(f32[64,128]{1,0:T(8,128)S(1)} %slice.36), channel_id=1, source_target_pairs={{0,1},{1,2},{2,3},{3,4},{4,5},{5,6},{6,7},{7,0},{8,9},{9,10},{10,1... | collective-permute-start | bytes 98312 | tf_op jit(solution)/shard_map/ppermute | solution.py:224
  131.3 25.2 %collective-permute-start.23 = (f32[64,128]{1,0:T(8,128)S(1)}, f32[64,128]{1,0:T(8,128)S(1)}, u32[]{:S(2)}, u32[]{:S(2)}) collective-permute-start(f32[64,128]{1,0:T(8,128)S(1)} %slice.36), channel_id=1, source_target_pairs={{0,7},{1,0},{2,1},{3,2},{4,3},{5,4},{6,5},{7,6},{8,15},{9,8},{10,9... | collective-permute-start | bytes 98312 | tf_op jit(solution)/shard_map/ppermute | solution.py:224
  148.5 8.0 %collective-permute-start.15 = (f32[64,128]{1,0:T(8,128)S(1)}, f32[64,128]{1,0:T(8,128)S(1)}, u32[]{:S(2)}, u32[]{:S(2)}) collective-permute-start(f32[64,128]{1,0:T(8,128)S(1)} %slice.35), channel_id=1, source_target_pairs={{0,1},{1,2},{2,3},{3,4},{4,5},{5,6},{6,7},{7,0},{8,9},{9,10},{10,1... | collective-permute-start | bytes 98312 | tf_op jit(solution)/shard_map/ppermute | solution.py:224
  148.6 7.9 %collective-permute-start.16 = (f32[64,128]{1,0:T(8,128)S(1)}, f32[64,128]{1,0:T(8,128)S(1)}, u32[]{:S(2)}, u32[]{:S(2)}) collective-permute-start(f32[64,128]{1,0:T(8,128)S(1)} %slice.35), channel_id=1, source_target_pairs={{0,7},{1,0},{2,1},{3,2},{4,3},{5,4},{6,5},{7,6},{8,15},{9,8},{10,9... | collective-permute-start | bytes 98312 | tf_op jit(solution)/shard_map/ppermute | solution.py:224
  151.8 4.6 %collective-permute-start.24 = (f32[32,128]{1,0:T(8,128)S(1)}, f32[32,128]{1,0:T(8,128)S(1)}, u32[]{:S(2)}, u32[]{:S(2)}) collective-permute-start(f32[32,128]{1,0:T(8,128)S(1)} %slice.37), channel_id=1, source_target_pairs={{0,6},{1,7},{2,0},{3,1},{4,2},{5,3},{6,4},{7,5},{8,14},{9,15},{10,... | collective-permute-start | bytes 49160 | tf_op jit(solution)/shard_map/ppermute | solution.py:224
